TPU v7x, 128 devices: a whole 4x4x4 slice. The times are simulated.
128 devices in a mesh: flow: 32 (over z, x, core), grp: 4 (over y).
Axes of the slice: x: 4, y: 4, z: 4, core: 2. Of those that a mesh axis runs over, the one named last changes fastest.
Arguments:
- velocity: float32 [3, 256, 32, 128], P(None, 'flow', 'grp'), may hold values from -6 to 6
- column_slot: int32 [256, 32], P('flow', 'grp'), may hold values from 0 to 2047, as said below
- scalars: float32 [32, 1048576], P(None, ('flow', 'grp')), may hold values from -6 to 6
- mass: float32 [1048576], P(('flow', 'grp')), may hold values from 0.5 to 2
- pair_weight: float32 [1048576], P(('flow', 'grp')), may hold values from 0.25 to 2
- particle_cell: int32 [1048576], P(('flow', 'grp')), may hold values from 0 to 8191
- mix_partner: int32 [1048576], P(('flow', 'grp')), may hold values from 0 to 8191
- migrate_to: int32 [1048576, 1], P(('flow', 'grp')), may hold values from 0 to 31; in each aligned block of 8192 rows (0 to 8191, 8192 to 16383, ...) at most 512 rows name the same one
- rate_matrix: float32 [32, 32], replicated, may hold values from -1 to 1
- enthalpy: float32 [32], replicated, may hold values from -1 to 1
Outputs:
- cell_energy: float32 [256, 32, 128], P('flow', 'grp')
- cell_density: float32 [256, 32, 128], P('flow', 'grp')
- moved_scalars: float32 [32, 2097152], P(None, ('flow', 'grp'))
- moved_mass: float32 [2097152], P(('flow', 'grp'))
Inputs may be any that keep to these rules, and one draw needn't show every extreme that they name: `column_slot`: for each grp index g the values of the columns y with y // 8 == g form a permutation of 0 to 2047. The 64 columns of one device send at most 4 columns to one partition v // 64, and some device sends exactly 4 to some partition in every draw. `particle_cell`: index into the cells of the particle's own device, position * 128 + z. `mix_partner`: index of the partner among the particles of the same device. `migrate_to`: among the 8192 particles of one device at most 512 name one partition, and that bound is reached in every draw.
All inputs are finite; a program needn't handle non-finite values.
Results may differ from a plain program's by a relative error of at most 0.0003.
Values sent between devices are 32-bit elements; how exact they have to be, the bound alone decides.
A program may use at most 64 MiB of HBM per device.

v0:
```python
import jax
import jax.numpy as jnp
from jax import lax
from jax.sharding import PartitionSpec as P

mix_step = 0.5
react_step = 0.5


def padded_2(cells, sides, width):
    for axis, dim in sides:
        count = lax.axis_size(axis)
        ends = count - 1
        head = lax.slice_in_dim(cells, 0, width, axis=dim)
        tail = lax.slice_in_dim(cells, cells.shape[dim] - width, cells.shape[dim], axis=dim)
        cells = jnp.concatenate(
            [
                lax.ppermute(tail, axis, [(i, (i + 1) % count) for i in range(ends)]),
                cells,
                lax.ppermute(head, axis, [((i + 1) % count, i) for i in range(ends)]),
            ],
            axis=dim,
        )
    return cells


def block_rank(labels, classes):
    total_rows = labels.shape[0]
    block_rows = min(512, total_rows)
    blocks = total_rows // block_rows
    onehot = (labels[:, None] == jnp.arange(classes, dtype=jnp.int32)[None, :]).astype(jnp.bfloat16)
    onehot = onehot.reshape(blocks, block_rows, classes)
    lower_ones = (jnp.arange(block_rows)[:, None] > jnp.arange(block_rows)[None, :]).astype(
        jnp.bfloat16
    )
    within = jnp.einsum("ij,bjc->bic", lower_ones, onehot, preferred_element_type=jnp.float32)
    totals = jnp.sum(onehot.astype(jnp.float32), axis=1)
    offsets = jnp.cumsum(totals, axis=0) - totals
    place_rank = jnp.sum((within + offsets[:, None, :]) * onehot.astype(jnp.float32), axis=2)
    return place_rank.reshape(total_rows).astype(jnp.int32)


def per_device(
    velocity,
    column_slot,
    scalars,
    mass,
    pair_weight,
    particle_cell,
    mix_partner,
    migrate_to,
    rate_matrix,
    enthalpy,
):
    flows = lax.axis_size("flow")
    width_x = velocity.shape[1]
    width_y = velocity.shape[2]
    depth = velocity.shape[3]
    columns = width_x * width_y
    particles = scalars.shape[1]
    capacity = 2 * columns // flows
    most_rows = 2 * particles // flows
    padded = padded_2(velocity, (("flow", 1), ("grp", 2)), 1)
    padded = jnp.pad(padded, ((0, 0), (0, 0), (0, 0), (1, 1)))
    diff_x = padded[:, 2:, 1:-1, 1:-1] - padded[:, :-2, 1:-1, 1:-1]
    diff_y = padded[:, 1:-1, 2:, 1:-1] - padded[:, 1:-1, :-2, 1:-1]
    diff_z = padded[:, 1:-1, 1:-1, 2:] - padded[:, 1:-1, 1:-1, :-2]
    strain = jnp.sum(diff_x * diff_x + diff_y * diff_y + diff_z * diff_z, axis=0) * 0.25
    omega = 0.5 + 0.25 * jnp.sqrt(strain)
    column_values = column_slot.reshape(columns)
    target = column_values // columns
    send_index = target * capacity + block_rank(target, flows)
    fields = jnp.concatenate([omega[None], velocity], axis=0).reshape(4, columns, depth)
    outgoing = jnp.zeros((4, flows * capacity, depth), jnp.float32).at[:, send_index].set(fields)
    arrived = lax.all_to_all(outgoing, "flow", split_axis=1, concat_axis=1, tiled=True)
    every_slot = lax.all_gather(column_values, "flow", axis=0, tiled=True).reshape(flows, columns)
    own_part = lax.axis_index("flow")
    matches = (every_slot // columns == own_part).astype(jnp.int32)
    match_rank = jnp.cumsum(matches, axis=1) - matches
    source_row = jnp.arange(flows, dtype=jnp.int32)[:, None]
    slot_of = jnp.where(matches == 1, source_row * capacity + match_rank, flows * capacity)
    lookup = jnp.full((flows * capacity,), columns, jnp.int32)
    lookup = lookup.at[slot_of.reshape(-1)].set((every_slot % columns).reshape(-1), mode="drop")
    placed = (
        jnp.zeros((arrived.shape[0], columns, depth), jnp.float32)
        .at[:, lookup]
        .set(arrived, mode="drop")
    )
    cell_column = particle_cell // depth
    cell_depth = particle_cell % depth
    column_hot = (cell_column[:, None] == jnp.arange(columns, dtype=jnp.int32)[None, :]).astype(
        jnp.float32
    )
    depth_hot = (cell_depth[:, None] == jnp.arange(depth, dtype=jnp.int32)[None, :]).astype(
        jnp.float32
    )

    def read_field(field):
        rows = jnp.dot(column_hot, field, precision=lax.Precision.HIGHEST)
        return jnp.sum(rows * depth_hot, axis=1)

    at_cell = lax.map(read_field, placed)
    omega_part = at_cell[0]
    kinetic_part = 0.5 * jnp.sum(at_cell[1:] * at_cell[1:], axis=0)
    scalar_rows = scalars.T
    partner = jnp.take(scalar_rows, mix_partner, axis=0).T
    fraction = 1.0 - jnp.exp(-mix_step * pair_weight * omega_part)
    mixed = scalars + fraction[None, :] * (partner - scalars)
    rate = jnp.dot(rate_matrix, mixed, precision=lax.Precision.HIGHEST)
    reacted = mixed + react_step * jnp.tanh(rate)
    energy = jnp.dot(enthalpy, reacted, precision=lax.Precision.HIGHEST) + kinetic_part
    weighted = jnp.concatenate(
        [(mass * energy)[:, None] * depth_hot, mass[:, None] * depth_hot], axis=1
    )
    binned_cells = jnp.dot(column_hot.T, weighted, precision=lax.Precision.HIGHEST)
    bins = jnp.transpose(binned_cells.reshape(columns, 2, depth), (1, 0, 2))
    filled = (lookup < columns).astype(jnp.float32)
    back_rows = jnp.take(bins, jnp.minimum(lookup, columns - 1), axis=1) * filled[None, :, None]
    target_part = migrate_to[:, 0]
    move_index = target_part * most_rows + block_rank(target_part, flows)
    source_of = jnp.full((flows * most_rows,), particles, jnp.int32)
    source_of = source_of.at[move_index].set(jnp.arange(particles, dtype=jnp.int32))
    particle_rows = jnp.concatenate([reacted.T, mass[:, None]], axis=1)
    particle_rows = jnp.concatenate(
        [particle_rows, jnp.zeros((1, particle_rows.shape[1]), jnp.float32)], axis=0
    )
    picked = jnp.take(particle_rows, source_of, axis=0).T
    send_scalars = picked[:-1]
    send_mass = picked[-1:]
    returned = lax.all_to_all(back_rows, "flow", split_axis=1, concat_axis=1, tiled=True)
    moved_scalars, moved_mass = (
        lax.all_to_all(send_scalars, "flow", split_axis=1, concat_axis=1, tiled=True),
        lax.all_to_all(send_mass, "flow", split_axis=1, concat_axis=1, tiled=True),
    )
    binned = returned[:, send_index].reshape(2, width_x, width_y, depth)
    return (binned[0], binned[1], moved_scalars, moved_mass[0])


def solution(mesh):
    placed = (
        P(None, "flow", "grp", None),
        P("flow", "grp"),
        P(None, ("flow", "grp")),
        P(("flow", "grp")),
        P(("flow", "grp")),
        P(("flow", "grp")),
        P(("flow", "grp")),
        P(("flow", "grp"), None),
        P(),
        P(),
    )
    return jax.shard_map(
        per_device,
        mesh=mesh,
        in_specs=placed,
        out_specs=(
            P("flow", "grp", None),
            P("flow", "grp", None),
            P(None, ("flow", "grp")),
            P(("flow", "grp")),
        ),
        check_vma=False,
    )
```

profile of v0, /device:TPU:1, one launch (start us, length us, event | category | flops | bytes accessed | tf_op | source)
XLA Modules:
  0.0 305.2 jit_solution(13261118814173290705)
XLA Ops:
  1.5 3.3 %collective-permute-start = (f32[3,1,8,128]{3,2,1,0:T(8,128)S(1)}, f32[3,1,8,128]{3,2,1,0:T(8,128)S(1)}, u32[]{:S(2)}, u32[]{:S(2)}) collective-permute-start(f32[3,1,8,128]{3,2,1,0:T(8,128)S(1)} %get-tuple-element.91), channel_id=1, source_target_pairs={{4,0},{8,4},{12,8},{16,12},{20,16},{24,20},{28,24},{32,28},{36,32}... | collective-permute-start | bytes 36872 | tf_op jit(solution)/shard_map/ppermute | solution.py:20
  4.8 3.1 %collective-permute-start.1 = (f32[3,1,8,128]{3,2,1,0:T(8,128)S(1)}, f32[3,1,8,128]{3,2,1,0:T(8,128)S(1)}, u32[]{:S(2)}, u32[]{:S(2)}) collective-permute-start(f32[3,1,8,128]{3,2,1,0:T(8,128)S(1)} %get-tuple-element.92), channel_id=1, source_target_pairs={{0,4},{4,8},{8,12},{12,16},{16,20},{20,24},{24,28},{28,32},{32,36}... | collective-permute-start | bytes 36872 | tf_op jit(solution)/shard_map/ppermute | solution.py:18
  11.5 1.5 reduce.7
  14.7 30.5 %scatter_custom_fusion.3 = s32[16384]{0:T(1024)S(1)} fusion(s32[8192]{0:T(1024)S(1)} %bitcast.122, s32[8192]{0:T(1024)S(1)} %iota.52, s32[]{:T(128)} %constant.159.clone.1), kind=kCustom, calls=%fused_computation.88 | custom fusion | bytes 65540 | tf_op jit(solution)/shard_map/scatter | solution.py:122
  47.9 14.4 %all-reduce.2 = s32[2048]{0:T(1024)S(1)} all-reduce(s32[2048]{0:T(1024)S(1)} %dynamic-update-slice), channel_id=1, replica_groups=mesh['flow'=32,'grp'=4] {'flow'}, use_global_device_ids=true, to_apply=%add.2 | all-reduce | flops 2048 | bytes 16384
  62.9 8.0 %scatter_custom_fusion = s32[128]{0:T(128)S(1)} fusion(s32[2048]{0:T(1024)S(1)} %get-tuple-element.100, s32[2048]{0:T(1024)S(1)} %get-tuple-element.99, s32[]{:T(128)} %constant.142.clone.1), kind=kCustom, calls=%fused_computation.151 | custom fusion | bytes 516 | tf_op jit(solution)/shard_map/scatter | solution.py:83
  71.9 3.2 %collective-permute-start.3 = (f32[3,10,1,128]{3,2,1,0:T(1,128)S(1)}, f32[3,10,1,128]{3,2,1,0:T(1,128)S(1)}, u32[]{:S(2)}, u32[]{:S(2)}) collective-permute-start(f32[3,10,1,128]{3,2,1,0:T(1,128)S(1)} %get-tuple-element.89), channel_id=1, source_target_pairs={{0,1},{1,2},{2,3},{4,5},{5,6},{6,7},{8,9},{9,10},{10,11},{12,13},{... | collective-permute-start | bytes 46088 | tf_op jit(solution)/shard_map/ppermute | solution.py:18
  77.4 2.2 collective-permute-done.2
  80.9 6.9 %scatter_fusion = f32[4,128,128]{2,0,1:T(4,128)} fusion(f32[4,128,128]{2,0,1:T(4,128)} %broadcast_in_dim.94, s32[64]{0:T(128)S(1)} %fusion.66, f32[64,4,128]{2,1,0:T(4,128)S(1)} %maximum_bitcast_fusion), kind=kCustom, calls=%fused_computation.5 | custom fusion | bytes 393472 | tf_op jit(solution)/shard_map/scatter | solution.py:74
  87.8 8.7 %all-to-all-start = ((f32[4,128,128]{2,0,1:T(4,128)}), f32[4,128,128]{2,0,1:T(4,128)S(1)}, u32[]{:S(2)}, u32[]{:S(2)}) async-start(f32[4,128,128]{2,0,1:T(4,128)} %scatter_fusion), calls=%async_computation | async-start | bytes 524288 | tf_op jit(solution)/shard_map/all_to_all | solution.py:75
  96.5 2.6 copy.51
  99.1 29.9 %gather_fusion = f32[8192,32]{1,0:T(8,128)} fusion(f32[8192,32]{1,0:T(8,128)} %bitcast.105, s32[8192]{0:T(1024)S(1)} %fusion.52), kind=kCustom, calls=%fused_computation | custom fusion | bytes 2129920 | tf_op jit(solution)/shard_map/jit(_take)/gather | solution.py:106
  129.0 2.8 copy.52
  131.9 4.6 %scatter_fusion.1 = f32[4,64,128]{2,0,1:T(4,128)S(1)} fusion(f32[4,64,128]{2,0,1:T(4,128)S(1)} %broadcast_in_dim.92, s32[128]{0:T(128)S(1)} %compare_select_fusion.5, f32[128,4,128]{2,1,0:T(4,128)S(1)} %bitcast.110), kind=kCustom, calls=%fused_computation.6 | custom fusion | bytes 786944 | tf_op jit(solution)/shard_map/scatter | solution.py:87
  136.5 18.5 %while.11 = (s32[]{:T(128)}, f32[4,8192]{1,0:T(4,128)S(1)}, f32[4,64,128]{2,0,1:T(4,128)S(1)}, s32[8192]{0:T(1024)S(1)}, s32[8192]{0:T(1024)S(1)}, /*index=5*/s32[]{:T(128)}, s32[]{:T(128)}) while((s32[]{:T(128)}, f32[4,8192]{1,0:T(4,128)S(1)}, f32[4,64,128]{2,0,1:T(4,128)S(1)}, s32[8192]{0:T(1024)S(1)}, s32[8192]{0:T(1024)S(1)}, ...), condition=%wide.region_9.10_spmd.clone, body=%wide.region_7.9_spmd.clone.sunk | while | flops 809492480 | bytes 262237 | solution.py:102
  136.6 4.1 %fusion.84 = f32[8192]{0:T(1024)S(1)} fusion(f32[64,128]{1,0:T(8,128)S(1)} %bitcast.113, s32[8192]{0:T(1024)S(1)} %get-tuple-element.151, s32[8192]{0:T(1024)S(1)} %get-tuple-element.150), kind=kOutput, calls=%fused_computation.15.clone.1 | convolution fusion | flops 809492480 | bytes 131072 | tf_op jit(solution)/shard_map/while/body/eval_jaxpr/dot_general | solution.py:99
  141.2 4.1 %fusion.84 = f32[8192]{0:T(1024)S(1)} fusion(f32[64,128]{1,0:T(8,128)S(1)} %bitcast.113, s32[8192]{0:T(1024)S(1)} %get-tuple-element.151, s32[8192]{0:T(1024)S(1)} %get-tuple-element.150), kind=kOutput, calls=%fused_computation.15.clone.1 | convolution fusion | flops 809492480 | bytes 131072 | tf_op jit(solution)/shard_map/while/body/eval_jaxpr/dot_general | solution.py:99
  145.8 4.1 %fusion.84 = f32[8192]{0:T(1024)S(1)} fusion(f32[64,128]{1,0:T(8,128)S(1)} %bitcast.113, s32[8192]{0:T(1024)S(1)} %get-tuple-element.151, s32[8192]{0:T(1024)S(1)} %get-tuple-element.150), kind=kOutput, calls=%fused_computation.15.clone.1 | convolution fusion | flops 809492480 | bytes 131072 | tf_op jit(solution)/shard_map/while/body/eval_jaxpr/dot_general | solution.py:99
  150.4 4.1 %fusion.84 = f32[8192]{0:T(1024)S(1)} fusion(f32[64,128]{1,0:T(8,128)S(1)} %bitcast.113, s32[8192]{0:T(1024)S(1)} %get-tuple-element.151, s32[8192]{0:T(1024)S(1)} %get-tuple-element.150), kind=kOutput, calls=%fused_computation.15.clone.1 | convolution fusion | flops 809492480 | bytes 131072 | tf_op jit(solution)/shard_map/while/body/eval_jaxpr/dot_general | solution.py:99
  157.3 2.7 copy.58
  160.1 3.7 %concatenate.43.clone = f32[8193,33]{1,0:T(8,128)} pad(f32[8192,33]{1,0:T(8,128)} %copy.58, f32[]{:T(128)} %constant.156.clone.1), padding=0_1x0_0 | pad | bytes 2162824 | tf_op jit(solution)/shard_map/concatenate | solution.py:124
  163.8 56.6 %gather_fusion.3 = f32[16384,33]{1,0:T(8,128)} fusion(f32[8193,33]{1,0:T(8,128)} %concatenate.43.clone, s32[16384]{0:T(1024)S(1)} %fusion.47), kind=kCustom, calls=%fused_computation.3 | custom fusion | bytes 4390912 | tf_op jit(solution)/shard_map/jit(_take)/gather | solution.py:127
  220.4 11.8 %select_bitcast_fusion = f32[33,16384]{0,1:T(8,128)S(1)} fusion(f32[16384,33]{1,0:T(8,128)} %gather_fusion.3, pred[16384]{0:T(1024)(128)(4,1)S(1)} %compare_and_fusion), kind=kLoop, calls=%fused_computation.27 | loop fusion | flops 540672 | bytes 4341760 | tf_op jit(solution)/shard_map/jit(_take)/select_n | solution.py:127
  232.1 5.2 %slice_reduce_fusion = f32[16384]{0:T(1024)} fusion(f32[33,16384]{0,1:T(8,128)S(1)} %select_bitcast_fusion), kind=kLoop, calls=%fused_computation.22 | loop fusion | bytes 131072 | tf_op jit(solution)/shard_map/slice | solution.py:129
  237.3 7.4 %all-to-all-start.3 = ((f32[1,32,512]{2,0,1:T(1,128)}), f32[1,32,512]{2,0,1:T(1,128)S(1)}, u32[]{:S(2)}, u32[]{:S(2)}) async-start(f32[1,32,512]{2,0,1:T(1,128)} %bitcast.31), calls=%async_computation.3 | async-start | bytes 131072 | tf_op jit(solution)/shard_map/all_to_all | solution.py:133
  244.7 3.4 %fusion.17 = (f32[8192,128]{1,0:T(8,128)S(1)}, f32[8192,128]{1,0:T(8,128)S(1)}) fusion(f32[8192]{0:T(1024)S(1)} %add_multiply_fusion, s32[8192]{0:T(1024)S(1)} %get-tuple-element.167, f32[8192]{0:T(1024)S(1)} %copy-done.4), kind=kLoop, calls=%fused_computation.29 | loop fusion | flops 3145728 | bytes 8486912 | tf_op jit(solution)/shard_map/mul | solution.py:113
  248.1 3.5 %fusion.13 = f32[64,256]{1,0:T(8,128)S(1)} fusion(f32[8192,128]{1,0:T(8,128)S(1)} %get-tuple-element.96, f32[8192,128]{1,0:T(8,128)S(1)} %get-tuple-element.95, s32[8192]{0:T(1024)S(1)} %get-tuple-element.166), kind=kOutput, calls=%fused_computation.23 | convolution fusion | flops 1613234176 | bytes 8486912 | tf_op jit(solution)/shard_map/dot_general | solution.py:115
  253.4 7.4 %all-to-all-start.1 = ((f32[2,128,128]{2,0,1:T(2,128)}), f32[2,128,128]{2,0,1:T(2,128)S(1)}, u32[]{:S(2)}, u32[]{:S(2)}) async-start(f32[2,128,128]{2,0,1:T(2,128)} %multiply_bitcast_fusion), calls=%async_computation.1 | async-start | bytes 262144 | tf_op jit(solution)/shard_map/all_to_all | solution.py:130
  260.8 6.2 %copy.54 = f32[32,32,512]{2,0,1:T(8,128)} copy(f32[32,32,512]{0,2,1:T(8,128)} %bitcast.106) | data formatting | bytes 4194304 | tf_op jit(solution)/shard_map/all_to_all | solution.py:132
  268.4 6.0 %all-to-all-start.2 = ((f32[32,32,512]{2,0,1:T(8,128)}), f32[32,32,512]{2,0,1:T(8,128)S(1)}, u32[]{:S(2)}, u32[]{:S(2)}) async-start(f32[32,32,512]{2,0,1:T(8,128)} %copy.54), calls=%async_computation.2 | async-start | bytes 4194304 | tf_op jit(solution)/shard_map/all_to_all | solution.py:132
  275.8 27.2 %all-to-all-done.2 = f32[32,32,512]{2,0,1:T(8,128)S(1)} async-done(((f32[32,32,512]{2,0,1:T(8,128)}), f32[32,32,512]{2,0,1:T(8,128)S(1)}, u32[]{:S(2)}, u32[]{:S(2)}) %all-to-all-start.2) | async-done | bytes 2097184 | tf_op jit(solution)/shard_map/all_to_all | solution.py:132
  303.0 1.5 copy.59
  (94 shorter events, 22.6 us)
Async XLA Ops:
  0.6 154.6 %copy-start = (f32[32,32]{1,0:T(8,128)S(1)}, f32[32,32]{1,0:T(8,128)}, u32[]{:S(2)}) copy-start(f32[32,32]{1,0:T(8,128)} %param.20) | copy-start | bytes 12292
  0.6 79.3 %copy-start.3 = (f32[3,8,8,128]{3,2,1,0:T(8,128)S(1)}, f32[3,8,8,128]{3,2,1,0:T(8,128)}, u32[]{:S(2)}) copy-start(f32[3,8,8,128]{3,2,1,0:T(8,128)} %param.12) | copy-start | bytes 294916
  0.7 95.8 %copy-start.2 = (f32[32,8192]{1,0:T(8,128)S(1)}, f32[32,8192]{1,0:T(8,128)}, u32[]{:S(2)}) copy-start(f32[32,8192]{1,0:T(8,128)} %param.14) | copy-start | bytes 3145732
  1.5 70.4 %collective-permute-start = (f32[3,1,8,128]{3,2,1,0:T(8,128)S(1)}, f32[3,1,8,128]{3,2,1,0:T(8,128)S(1)}, u32[]{:S(2)}, u32[]{:S(2)}) collective-permute-start(f32[3,1,8,128]{3,2,1,0:T(8,128)S(1)} %get-tuple-element.91), channel_id=1, source_target_pairs={{4,0},{8,4},{12,8},{16,12},{20,16},{24,20},{28,24},{32,28},{36,32}... | collective-permute-start | bytes 36872 | tf_op jit(solution)/shard_map/ppermute | solution.py:20
  4.8 66.2 %collective-permute-start.1 = (f32[3,1,8,128]{3,2,1,0:T(8,128)S(1)}, f32[3,1,8,128]{3,2,1,0:T(8,128)S(1)}, u32[]{:S(2)}, u32[]{:S(2)}) collective-permute-start(f32[3,1,8,128]{3,2,1,0:T(8,128)S(1)} %get-tuple-element.92), channel_id=1, source_target_pairs={{0,4},{4,8},{8,12},{12,16},{16,20},{20,24},{24,28},{28,32},{32,36}... | collective-permute-start | bytes 36872 | tf_op jit(solution)/shard_map/ppermute | solution.py:18
  71.9 5.5 %collective-permute-start.3 = (f32[3,10,1,128]{3,2,1,0:T(1,128)S(1)}, f32[3,10,1,128]{3,2,1,0:T(1,128)S(1)}, u32[]{:S(2)}, u32[]{:S(2)}) collective-permute-start(f32[3,10,1,128]{3,2,1,0:T(1,128)S(1)} %get-tuple-element.89), channel_id=1, source_target_pairs={{0,1},{1,2},{2,3},{4,5},{5,6},{6,7},{8,9},{9,10},{10,11},{12,13},{... | collective-permute-start | bytes 46088 | tf_op jit(solution)/shard_map/ppermute | solution.py:18
  75.1 4.5 %collective-permute-start.2 = (f32[3,10,1,128]{3,2,1,0:T(1,128)S(1)}, f32[3,10,1,128]{3,2,1,0:T(1,128)S(1)}, u32[]{:S(2)}, u32[]{:S(2)}) collective-permute-start(f32[3,10,1,128]{3,2,1,0:T(1,128)S(1)} %get-tuple-element.90), channel_id=1, source_target_pairs={{1,0},{2,1},{3,2},{5,4},{6,5},{7,6},{9,8},{10,9},{11,10},{13,12},{... | collective-permute-start | bytes 46088 | tf_op jit(solution)/shard_map/ppermute | solution.py:20
  87.8 44.1 %all-to-all-start = ((f32[4,128,128]{2,0,1:T(4,128)}), f32[4,128,128]{2,0,1:T(4,128)S(1)}, u32[]{:S(2)}, u32[]{:S(2)}) async-start(f32[4,128,128]{2,0,1:T(4,128)} %scatter_fusion), calls=%async_computation | async-start | bytes 524288 | tf_op jit(solution)/shard_map/all_to_all | solution.py:75
  129.0 2.8 copy-start.5
  136.5 18.7 %copy-start.6 = (f32[8192]{0:T(1024)S(1)}, f32[8192]{0:T(1024)}, u32[]{:S(2)}) copy-start(f32[8192]{0:T(1024)} %param.16) | copy-start | bytes 98308
  136.5 20.1 %copy-start.7 = (f32[32]{0:T(128)S(1)}, f32[32]{0:T(128)}, u32[]{:S(2)}) copy-start(f32[32]{0:T(128)} %param.21) | copy-start | bytes 388
  155.0 2.2 copy-start.4
  232.1 5.2 %copy-start.1 = (f32[33,16384]{0,1:T(8,128)}, f32[33,16384]{0,1:T(8,128)S(1)}, u32[]{:S(2)}) copy-start(f32[33,16384]{0,1:T(8,128)S(1)} %select_bitcast_fusion) | copy-start | bytes 6488068
  237.3 16.1 %all-to-all-start.3 = ((f32[1,32,512]{2,0,1:T(1,128)}), f32[1,32,512]{2,0,1:T(1,128)S(1)}, u32[]{:S(2)}, u32[]{:S(2)}) async-start(f32[1,32,512]{2,0,1:T(1,128)} %bitcast.31), calls=%async_computation.3 | async-start | bytes 131072 | tf_op jit(solution)/shard_map/all_to_all | solution.py:133
  253.4 15.0 %all-to-all-start.1 = ((f32[2,128,128]{2,0,1:T(2,128)}), f32[2,128,128]{2,0,1:T(2,128)S(1)}, u32[]{:S(2)}, u32[]{:S(2)}) async-start(f32[2,128,128]{2,0,1:T(2,128)} %multiply_bitcast_fusion), calls=%async_computation.1 | async-start | bytes 262144 | tf_op jit(solution)/shard_map/all_to_all | solution.py:130
  268.4 34.6 %all-to-all-start.2 = ((f32[32,32,512]{2,0,1:T(8,128)}), f32[32,32,512]{2,0,1:T(8,128)S(1)}, u32[]{:S(2)}, u32[]{:S(2)}) async-start(f32[32,32,512]{2,0,1:T(8,128)} %copy.54), calls=%async_computation.2 | async-start | bytes 4194304 | tf_op jit(solution)/shard_map/all_to_all | solution.py:132
where the time goes:
time: 307 us; the launch traced here: 305 us
  local copies, waits for them, and re-layouts  174 us (57%)
  starting transfers between devices  40.4 us (13%)
  waiting for transfers between devices  30.8 us (10%)
  matrix products  22.6 us (7%)
  other arithmetic  21.5 us (7%)
  blocking collectives  14.4 us (5%)
    gather x1, local copies, waits for them, and re-layouts, per_device(): picked = jnp.take(particle_rows, source_of, axis=0).T  56.6 us
    gather x2, local copies, waits for them, and re-layouts, per_device(): partner = jnp.take(scalar_rows, mix_partner, axis=0).T  32.7 us
    scatter x1, local copies, waits for them, and re-layouts, per_device(): source_of.at[move_index].set(jnp.arange(particles, dtype=jnp.int32))  30.5 us
    all_to_all x1, waiting for transfers between devices, per_device(): lax.all_to_all(send_scalars, 'flow', split_axis=1, concat_axis=1, tiled=T...  27.2 us
    dot_general x4, matrix products, read_field(): rows = jnp.dot(column_hot, field, precision=lax.Precision.HIGHEST)  16.2 us
    unnamed x1, blocking collectives  14.4 us
    select_n x1, other arithmetic, per_device(): picked = jnp.take(particle_rows, source_of, axis=0).T  11.8 us
    unnamed x26, local copies, waits for them, and re-layouts  8.99 us
  transfers between devices with their start and end apart: 8, of which 3 were waited for; matrix products, arithmetic and copies ran while one was open for 33% of the time, Pallas kernels for 0%

commit v1 on v0

v1 whole, which is shorter than its diff:
```python
import functools

import jax
import jax.numpy as jnp
from jax import lax
from jax.experimental import pallas as pl
from jax.experimental.pallas import tpu as pltpu
from jax.sharding import PartitionSpec as P

mix_step = 0.5
react_step = 0.5
MESH = pl.DeviceIdType.MESH
f32 = jnp.float32
bf16 = jnp.bfloat16
i32 = jnp.int32
HIGH = lax.Precision.HIGHEST

N = 32
NG = 4
PD = 8192
CH = PD // 128
CAP = 512
COLS = 64

_GROUPS = [
    [(2, 2)],
    [(1, 2), (3, 2), (2, 1), (2, 3)],
    [(1, 3), (3, 1)],
    [(1, 1), (3, 3)],
    [(0, 2), (2, 0)],
    [(0, 1), (0, 3), (1, 0), (3, 0)],
]
_ORDER = [(a, b, c) for g in _GROUPS for c in (0, 1) for (a, b) in g] + [(0, 0, 1)]
_CODES = [a * 8 + b * 2 + c for (a, b, c) in _ORDER]
_WORDS = [
    sum(code << (5 * j) for j, code in enumerate(_CODES[6 * w : 6 * w + 6]))
    for w in range(6)
]


def ordered_peer(t, me):
    w = t // 6
    word = jnp.int32(_WORDS[0])
    for j in range(1, 6):
        word = jnp.where(w == j, jnp.int32(_WORDS[j]), word)
    code = jnp.bitwise_and(jnp.right_shift(word, 5 * (t - 6 * w)), 31)
    z = lax.rem(me // 8 + code // 8, 4)
    x = lax.rem(lax.rem(me // 2, 4) + lax.rem(code // 2, 4), 4)
    c = lax.rem(me + code, 2)
    return (z * 4 + x) * 2 + c


def split2(x):
    hi = x.astype(bf16)
    lo = (x - hi.astype(f32)).astype(bf16)
    return hi, lo


def split3(x):
    hi = x.astype(bf16)
    r = x - hi.astype(f32)
    mid = r.astype(bf16)
    lo = (r - mid.astype(f32)).astype(bf16)
    return hi, mid, lo


def dot(a, b):
    return jnp.dot(a, b, preferred_element_type=f32)


def dot_nt(a, b):
    return lax.dot_general(a, b, (((1,), (1,)), ((), ())), preferred_element_type=f32)


def select_dot(hot, x):
    a, b, c = split3(x)
    return dot(hot, a) + dot(hot, b) + dot(hot, c)


def iota(shape, dim):
    return lax.broadcasted_iota(i32, shape, dim)


def kernel(
    vel_in, vrow_in, scal_in, mass_in, pw_in, cell_in, mig_in, part, rmat_in, enth_in,
    ce, cd, ms, mm,
    vel, vrow, scal, mass, pw, cell, mig, rmat, enth,
    hx, hy, ysnd, ypad, q2, q2t, wmat, possend, posrecv, fsend, frecv, bsend, brecv,
    rows, pt, gbuf, slot, srcv, mbuf, tab, frac, kinp, en, sendbuf,
    part_s, src_s,
    isem, lsem, hss, hrs, pss, prs, css, crs, mss, mrs, dss, drs, bss, brs,
):
    me = lax.axis_index("flow")
    g = lax.axis_index("grp")

    def peer(t):
        return lax.rem(me + t, N)

    loads = [
        pltpu.make_async_copy(src, dst, isem.at[k])
        for k, (src, dst) in enumerate(
            [
                (vrow_in, vrow), (vel_in, vel), (scal_in, scal), (mig_in, mig), (mass_in, mass),
                (pw_in, pw), (cell_in, cell), (rmat_in, rmat), (enth_in, enth), (part, part_s),
            ]
        )
    ]
    for copy in loads:
        copy.start()

    def remote(src, dst, ss, rs, dev):
        return pltpu.make_async_remote_copy(
            src_ref=src, dst_ref=dst, send_sem=ss, recv_sem=rs, device_id=dev, device_id_type=MESH
        )

    barrier = pltpu.get_barrier_semaphore()

    def greet(t, _):
        pl.semaphore_signal(barrier, inc=1, device_id=(peer(t), g), device_id_type=MESH)
        return 0

    lax.fori_loop(1, N, greet, 0)
    for s in (1, NG - 1):
        pl.semaphore_signal(
            barrier, inc=1, device_id=(me, lax.rem(g + s, NG)), device_id_type=MESH
        )
    loads[0].wait()

    v = vrow[0:1, :]
    lane1 = iota((1, 128), 1)
    field = jnp.right_shift(lane1, 6)
    target = jnp.right_shift(v, 6)
    place = jnp.bitwise_and(v, 63) + 64 * field
    key = jnp.broadcast_to((target + 64 * field).astype(f32), (128, 128))
    earlier = jnp.where(
        jnp.logical_and(key.T == key, iota((128, 128), 0) < iota((128, 128), 1)), 1.0, 0.0
    )
    rank = jnp.sum(earlier, axis=0, keepdims=True).astype(i32)
    sidx = target * 8 + field * 4 + rank
    q2v = jnp.where(iota((256, 128), 0) == sidx, 1.0, 0.0).astype(bf16)
    q2[...] = q2v
    sidx_t = jnp.broadcast_to(sidx.astype(f32), (128, 128)).T.astype(i32)
    for h in range(2):
        q2t[:, 128 * h : 128 * h + 128] = jnp.where(
            iota((128, 128), 1) + 128 * h == sidx_t, 1.0, 0.0
        ).astype(bf16)
    place_t = jnp.broadcast_to((place + 1).astype(f32), (128, 128)).T.astype(bf16)
    possend[...] = dot(q2v, place_t) - 1.0
    loads[1].wait()
    for c in range(3):
        for x in range(8):
            ysnd[0, c, x : x + 1, :] = vel[c, x, 0:1, :]
            ysnd[1, c, x : x + 1, :] = vel[c, x, 7:8, :]

    pl.semaphore_wait(barrier, N - 1 + 2)

    nxt, prv = lax.rem(me + 1, N), lax.rem(me + N - 1, N)
    gn, gp = lax.rem(g + 1, NG), lax.rem(g + NG - 1, NG)
    halo = [
        remote(vel.at[:, 7], hx.at[0], hss.at[0], hrs.at[0], (nxt, g)),
        remote(vel.at[:, 0], hx.at[1], hss.at[1], hrs.at[1], (prv, g)),
        remote(ysnd.at[1], hy.at[0], hss.at[2], hrs.at[2], (me, gn)),
        remote(ysnd.at[0], hy.at[1], hss.at[3], hrs.at[3], (me, gp)),
    ]
    for copy in halo:
        copy.start()

    def rows8(d):
        return pl.ds(pl.multiple_of(d * 8, 8), 8)

    def exchange(src, dst, ss, rs, own):
        def send(t, _):
            p = peer(t)
            remote(src.at[rows8(p)], dst.at[rows8(me)], ss.at[p], rs.at[me], (p, g)).start()
            return 0

        lax.fori_loop(1, N, send, 0)
        pltpu.make_async_copy(src.at[rows8(me)], dst.at[rows8(me)], own).start()

    def arrive(src, dst, ss, rs, own):
        def done(t, _):
            p = peer(t)
            copy = remote(src.at[rows8(p)], dst.at[rows8(p)], ss.at[p], rs.at[p], (p, g))
            copy.wait_send()
            copy.wait_recv()
            return 0

        lax.fori_loop(1, N, done, 0)
        pltpu.make_async_copy(src.at[rows8(me)], dst.at[rows8(me)], own).wait()

    exchange(possend, posrecv, pss, prs, lsem.at[1])

    loads[2].wait()

    def to_rows(c, _):
        col = pl.ds(pl.multiple_of(c * 128, 128), 128)
        x = scal[:, col]
        rows[col, :] = jnp.concatenate([x, x, x, x], axis=0).T
        return 0

    lax.fori_loop(0, CH // 2, to_rows, 0, unroll=8)

    for copy in halo:
        copy.wait()
    strain = jnp.zeros((64, 128), f32)
    square = jnp.zeros((64, 128), f32)
    lane64 = iota((64, 128), 1)
    for c in range(3):
        a = vel[c]
        left = jnp.where(me == 0, 0.0, hx[0, c])
        right = jnp.where(me == N - 1, 0.0, hx[1, c])
        down = jnp.where(g == 0, 0.0, hy[0, c])
        up = jnp.where(g == NG - 1, 0.0, hy[1, c])
        dx = jnp.concatenate([a[1:], right[None]], axis=0) - jnp.concatenate(
            [left[None], a[:-1]], axis=0
        )
        for x in range(8):
            ypad[x, 7:8, :] = down[x : x + 1, :]
            ypad[x, 8:16, :] = a[x]
            ypad[x, 16:17, :] = up[x : x + 1, :]
        dy = ypad[:, 9:17, :] - ypad[:, 7:15, :]
        flat = a.reshape(64, 128)
        dz = jnp.where(lane64 == 127, 0.0, pltpu.roll(flat, 127, 1)) - jnp.where(
            lane64 == 0, 0.0, pltpu.roll(flat, 1, 1)
        )
        dx = dx.reshape(64, 128)
        dy = dy.reshape(64, 128)
        strain = strain + (dx * dx + dy * dy + dz * dz)
        square = square + flat * flat
    omega = 0.5 + 0.25 * jnp.sqrt(strain * 0.25)
    both = jnp.concatenate([omega, 0.5 * square], axis=0)
    fsend[...] = select_dot(q2[...], both)
    exchange(fsend, frecv, css, crs, lsem.at[2])

    lax.fori_loop(CH // 2, CH, to_rows, 0, unroll=8)

    for copy in loads[3:9]:
        copy.wait()

    tri = jnp.concatenate(
        [
            jnp.where(iota((128, 128), 0) < iota((128, 128), 1), 1.0, 0.0).astype(bf16),
            jnp.ones((128, 128), bf16),
        ],
        axis=1,
    )

    def ranks(b, carry):
        hots = []
        for j in range(8):
            p = mig[pl.ds(b * 8 + j, 1), :]
            hots.append(jnp.where(iota((32, 128), 0) == p, 1.0, 0.0))
        hot = jnp.concatenate(hots, axis=0)
        pre = dot(hot.astype(bf16), tri)
        out = []
        for j in range(8):
            sl = slice(32 * j, 32 * j + 32)
            out.append(
                jnp.sum(hots[j] * (pre[sl, :128] + carry), axis=0, keepdims=True).astype(i32)
            )
            carry = carry + pre[sl, 128:]
        r8 = pl.ds(pl.multiple_of(b * 8, 8), 8)
        slot[r8, :] = mig[r8, :] * CAP + jnp.concatenate(out, axis=0)
        return carry

    lax.fori_loop(0, 8, ranks, jnp.zeros((32, 128), f32))

    def inverse(b, acc):
        left, right = [], []
        sub = iota((128, 128), 0)
        for j in range(4):
            c = b * 4 + j
            s = slot[pl.ds(c, 1), :]
            m = mass[pl.ds(c, 1), :]
            m_hi = m.astype(bf16).astype(f32)
            m_lo = m - m_hi
            left.append(jnp.where(sub == jnp.right_shift(s, 7), 1.0, 0.0).astype(bf16))
            at = sub == jnp.bitwise_and(s, 127)
            code = PD - c * 128 - lane1
            hi = jnp.right_shift(code, 7).astype(f32)
            lo = jnp.bitwise_and(code, 127).astype(f32)
            right.append(
                jnp.concatenate(
                    [jnp.where(at, w, 0.0).astype(bf16) for w in (hi, lo, m_hi, m_lo)], axis=0
                )
            )
        return acc + dot_nt(jnp.concatenate(left, axis=1), jnp.concatenate(right, axis=1))

    inv = lax.fori_loop(0, CH // 4, inverse, jnp.zeros((128, 512), f32))
    srcv[...] = jnp.clip((PD - (inv[:, 0:128] * 128.0 + inv[:, 128:256])).astype(i32), 0, PD)
    moved = inv[:, 256:384] + inv[:, 384:512]
    for p in range(N):
        mbuf[p] = moved[4 * p : 4 * p + 4, :]
    loads[9].wait()

    lanes = iota((1, 128), 1)
    quarter = [lanes < 32, lanes < 64, lanes < 96]

    def packed(index):
        a, b, c, d = [rows[pl.ds(index(q), 1), :] for q in range(4)]
        return jnp.where(quarter[1], jnp.where(quarter[0], a, b), jnp.where(quarter[2], c, d))

    def partners(b, _):
        for r in range(128):
            gbuf[r : r + 1, :] = packed(lambda q: part_s[4 * b + q, r])
        t = gbuf[...].T
        for q in range(4):
            col = pl.ds(pl.multiple_of(b * 512 + q * 128, 128), 128)
            pt[:, col] = t[32 * q : 32 * q + 32, :]
        return 0

    lax.fori_loop(0, 16, partners, 0)

    src_copy = pltpu.make_async_copy(srcv, src_s, lsem.at[3])
    src_copy.start()

    def send_mass(t, _):
        p = peer(t)
        remote(mbuf.at[p], mm.at[me], mss.at[p], mrs.at[me], (p, g)).start()
        return 0

    lax.fori_loop(1, N, send_mass, 0)
    own_mass = pltpu.make_async_copy(mbuf.at[me], mm.at[me], lsem.at[4])
    own_mass.start()

    arrive(possend, posrecv, pss, prs, lsem.at[1])
    pos = posrecv[...]
    wmat[...] = jnp.where(pos == iota((256, 128), 1).astype(f32), 1.0, 0.0).astype(bf16)
    wt = jnp.where(pos.T == iota((128, 256), 0).astype(f32), 1.0, 0.0).astype(bf16)
    arrive(fsend, frecv, css, crs, lsem.at[2])
    tab[...] = select_dot(wt, frecv[...])

    cz = [jnp.bitwise_and(cell[8 * k : 8 * k + 8, :], 127) for k in range(8)]
    cp = [jnp.right_shift(cell[8 * k : 8 * k + 8, :], 7) for k in range(8)]

    def lookup(n, acc):
        om = jnp.broadcast_to(tab[pl.ds(n, 1), :], (8, 128))
        ki = jnp.broadcast_to(tab[pl.ds(n + 64, 1), :], (8, 128))
        out = []
        for k in range(8):
            here = cp[k] == n
            out.append(jnp.where(here, jnp.take_along_axis(om, cz[k], axis=1), acc[2 * k]))
            out.append(jnp.where(here, jnp.take_along_axis(ki, cz[k], axis=1), acc[2 * k + 1]))
        return tuple(out)

    found = lax.fori_loop(0, 64, lookup, tuple(jnp.zeros((8, 128), f32) for _ in range(16)))
    for k in range(8):
        sl = slice(8 * k, 8 * k + 8)
        frac[sl, :] = 1.0 - jnp.exp(-mix_step * pw[sl, :] * found[2 * k])
        kinp[sl, :] = found[2 * k + 1]

    rates = rmat[...]
    forms = jnp.broadcast_to(enth[...], (8, 32))

    def react(b, _):
        mixed = []
        for j in range(4):
            c = b * 4 + j
            col = pl.ds(pl.multiple_of(c * 128, 128), 128)
            s = scal[:, col]
            mixed.append(s + frac[pl.ds(c, 1), :] * (pt[:, col] - s))
        mixed = jnp.concatenate(mixed, axis=1)
        rate = jnp.dot(rates, mixed, precision=HIGH, preferred_element_type=f32)
        out = mixed + react_step * jnp.tanh(rate)
        e = jnp.dot(forms, out, precision=HIGH, preferred_element_type=f32)
        for j in range(4):
            c = b * 4 + j
            en[pl.ds(c, 1), :] = e[0:1, 128 * j : 128 * j + 128] + kinp[pl.ds(c, 1), :]
            x = out[:, 128 * j : 128 * j + 128]
            col = pl.ds(pl.multiple_of(c * 128, 128), 128)
            rows[col, :] = jnp.concatenate([x, x, x, x], axis=0).T
        return 0

    lax.fori_loop(0, 16, react, 0)
    rows[PD : PD + 8, :] = jnp.zeros((8, 128), f32)
    src_copy.wait()

    def slots(d):
        return ms.at[:, pl.ds(pl.multiple_of(d * CAP, CAP), CAP)]

    def gather_block(p):
        for r in range(128):
            gbuf[r : r + 1, :] = packed(lambda q: src_s[4 * p + q, r])
        t = gbuf[...].T
        for q in range(4):
            sendbuf[p, :, 128 * q : 128 * q + 128] = t[32 * q : 32 * q + 32, :]

    def data(p, d):
        return remote(sendbuf.at[p], slots(d), dss.at[p], drs.at[d], (p, g))

    def send_data(t, _):
        p = ordered_peer(t, me)
        gather_block(p)
        remote(sendbuf.at[p], slots(me), dss.at[p], drs.at[me], (p, g)).start()
        return 0

    lax.fori_loop(0, 16, send_data, 0)

    def bins(b, acc):
        left, right = [], []
        sub = iota((128, 128), 0)
        sub64 = iota((64, 128), 0)
        for j in range(4):
            c = b * 4 + j
            w = cell[pl.ds(c, 1), :]
            m = mass[pl.ds(c, 1), :]
            e = m * en[pl.ds(c, 1), :]
            m_hi = m.astype(bf16).astype(f32)
            e_hi = e.astype(bf16).astype(f32)
            left.append(jnp.where(sub64 == jnp.right_shift(w, 7), 1.0, 0.0).astype(bf16))
            at = sub == jnp.bitwise_and(w, 127)
            right.append(
                jnp.concatenate(
                    [
                        jnp.where(at, y, 0.0).astype(bf16)
                        for y in (e_hi, e - e_hi, m_hi, m - m_hi)
                    ],
                    axis=0,
                )
            )
        return acc + dot_nt(jnp.concatenate(left, axis=1), jnp.concatenate(right, axis=1))

    sums = lax.fori_loop(0, CH // 4, bins, jnp.zeros((64, 512), f32))
    table = jnp.concatenate(
        [sums[:, 0:128] + sums[:, 128:256], sums[:, 256:384] + sums[:, 384:512]], axis=0
    )
    bsend[...] = select_dot(wmat[...], table)
    exchange(bsend, brecv, bss, brs, lsem.at[1])

    lax.fori_loop(16, N - 1, send_data, 0)
    gather_block(me)
    own = pltpu.make_async_copy(sendbuf.at[me], slots(me), lsem.at[5])
    own.start()

    arrive(bsend, brecv, bss, brs, lsem.at[1])
    back = select_dot(q2t[...], brecv[...])
    ce[...] = back[0:64, :]
    cd[...] = back[64:128, :]

    def finish(t, _):
        p = peer(t)
        copy = remote(mbuf.at[p], mm.at[p], mss.at[p], mrs.at[p], (p, g))
        copy.wait_send()
        copy.wait_recv()
        copy = data(p, p)
        copy.wait_send()
        copy.wait_recv()
        return 0

    lax.fori_loop(1, N, finish, 0)
    own_mass.wait()
    own.wait()


def per_device(
    velocity, column_slot, scalars, mass, pair_weight, particle_cell, mix_partner, migrate_to,
    rate_matrix, enthalpy,
):
    slots = column_slot.reshape(1, COLS)
    vrow = jnp.broadcast_to(jnp.concatenate([slots, slots], axis=1), (8, 128))
    vmem = pl.BlockSpec(memory_space=pltpu.VMEM)
    hbm = pl.BlockSpec(memory_space=pl.ANY)
    V = pltpu.VMEM
    D = pltpu.SemaphoreType.DMA
    ce, cd, ms, mm = pl.pallas_call(
        kernel,
        out_shape=(
            jax.ShapeDtypeStruct((64, 128), f32),
            jax.ShapeDtypeStruct((64, 128), f32),
            jax.ShapeDtypeStruct((32, N * CAP), f32),
            jax.ShapeDtypeStruct((N, 4, 128), f32),
        ),
        in_specs=[hbm] * 10,
        out_specs=(vmem, vmem, hbm, hbm),
        scratch_shapes=[
            V((3, 8, 8, 128), f32),
            V((8, 128), i32),
            V((32, PD), f32),
            V((CH, 128), f32),
            V((CH, 128), f32),
            V((CH, 128), i32),
            V((CH, 128), i32),
            V((32, 32), f32),
            V((1, 32), f32),
            V((2, 3, 8, 128), f32),
            V((2, 3, 8, 128), f32),
            V((2, 3, 8, 128), f32),
            V((8, 24, 128), f32),
            V((256, 128), bf16),
            V((128, 256), bf16),
            V((256, 128), bf16),
            V((256, 128), f32),
            V((256, 128), f32),
            V((256, 128), f32),
            V((256, 128), f32),
            V((256, 128), f32),
            V((256, 128), f32),
            V((PD + 8, 128), f32),
            V((32, PD), f32),
            V((128, 128), f32),
            V((CH, 128), i32),
            V((128, 128), i32),
            V((N, 4, 128), f32),
            V((128, 128), f32),
            V((CH, 128), f32),
            V((CH, 128), f32),
            V((CH, 128), f32),
            V((N, 32, CAP), f32),
            pltpu.SMEM((CH, 128), i32),
            pltpu.SMEM((128, 128), i32),
            D((10,)),
            D((6,)),
            D((4,)), D((4,)),
            D((N,)), D((N,)),
            D((N,)), D((N,)),
            D((N,)), D((N,)),
            D((N,)), D((N,)),
            D((N,)), D((N,)),
        ],
        compiler_params=pltpu.CompilerParams(
            collective_id=0, has_side_effects=True, vmem_limit_bytes=60 << 20
        ),
        name="step",
    )(
        velocity,
        vrow,
        scalars,
        mass.reshape(CH, 128),
        pair_weight.reshape(CH, 128),
        particle_cell.reshape(CH, 128),
        migrate_to.reshape(CH, 128),
        mix_partner.reshape(CH, 128),
        rate_matrix,
        enthalpy.reshape(1, 32),
    )
    return (ce.reshape(8, 8, 128), cd.reshape(8, 8, 128), ms, mm.reshape(N * CAP))


def solution(mesh):
    placed = (
        P(None, "flow", "grp", None),
        P("flow", "grp"),
        P(None, ("flow", "grp")),
        P(("flow", "grp")),
        P(("flow", "grp")),
        P(("flow", "grp")),
        P(("flow", "grp")),
        P(("flow", "grp"), None),
        P(),
        P(),
    )
    return jax.shard_map(
        per_device,
        mesh=mesh,
        in_specs=placed,
        out_specs=(
            P("flow", "grp", None),
            P("flow", "grp", None),
            P(None, ("flow", "grp")),
            P(("flow", "grp")),
        ),
        check_vma=False,
    )
```

time: 307 us -> 82.8 us (0.27)
  local copies, waits for them, and re-layouts: 174 us -> 7.83 us
  Pallas kernels: 0 us -> 74 us
  starting transfers between devices: 40.4 us -> 0 us
  waiting for transfers between devices: 30.8 us -> 0 us
  matrix products: 22.6 us -> 0 us
  other arithmetic: 21.5 us -> 0.08 us
  blocking collectives: 14.4 us -> 0 us
    gather x5 -> x0, local copies, waits for them, and re-layouts: 90.7 us -> none  [the longest x1 56.6 us: per_device(): picked = jnp.take(particle_rows, source_of, axis=0).T]
    pallas_call x0 -> x1, Pallas kernels: none -> 74 us  [per_device(): pl.pallas_call(kernel, out_shape=(jax.ShapeDtypeStruct((64, 128), f32), j...]
    scatter x4 -> x0, local copies, waits for them, and re-layouts: 50 us -> none  [the longest x1 30.5 us: per_device(): source_of.at[move_index].set(jnp.arange(particles, dtype=jnp.int32))]
    all_to_all x4 -> x0, starting transfers between devices: 29.5 us -> none  [the longest x1 8.65 us: per_device(): lax.all_to_all(outgoing, 'flow', split_axis=1, concat_axis=1, tiled=True)]
    all_to_all x4 -> x0, waiting for transfers between devices: 28.6 us -> none  [the longest x1 27.2 us: per_device(): lax.all_to_all(send_scalars, 'flow', split_axis=1, concat_axis=1, tiled=T...]
    dot_general x9 -> x0, matrix products: 22.6 us -> none  [the longest x4 16.2 us: read_field(): rows = jnp.dot(column_hot, field, precision=lax.Precision.HIGHEST)]
    unnamed x1 -> x0, blocking collectives: 14.4 us -> none
    select_n x7 -> x0, other arithmetic: 12.7 us -> none  [the longest x1 11.8 us: per_device(): picked = jnp.take(particle_rows, source_of, axis=0).T]
  transfers between devices with their start and end apart: 8 -> 0, of which waited for: 3 -> 0; matrix products, arithmetic and copies ran while one was open for 33% -> 0% of each run, Pallas kernels for 0% -> 0%
where the time goes in v1:
time: 82.8 us; the launch traced here: 82.5 us
  Pallas kernels  74 us (89%)
  local copies, waits for them, and re-layouts  7.83 us (9%)
    pallas_call x1, Pallas kernels, per_device(): pl.pallas_call(kernel, out_shape=(jax.ShapeDtypeStruct((64, 128), f32), j...  74 us
    unnamed x6, local copies, waits for them, and re-layouts  6.46 us

profile of v1, /device:TPU:1, one launch (start us, length us, event | category | flops | bytes accessed | tf_op | source)
XLA Modules:
  0.0 82.5 jit_solution(4714305034079554157)
XLA Ops:
  0.6 0.8 reshape.38
  1.4 0.1 add_bitcast_fusion
  1.5 0.6 broadcast_in_dim.8.vrow_in
  2.1 74.0 %step.1 = (f32[64,128]{1,0:T(8,128)}, f32[64,128]{1,0:T(8,128)}, f32[32,16384]{1,0:T(8,128)}, f32[32,4,128]{2,1,0:T(4,128)}) custom-call(f32[3,8,8,128]{3,2,1,0:T(8,128)} %vel_in.1, s32[8,128]{1,0:T(8,128)} %broadcast_in_dim.8.vrow_in, f32[32,8192]{1,0:T(8,128)} %scal_in.1, f32[64,128]{1,0:T(8,128)} %bitcast.12, f32[64,128]{1,0:T(8,128)} %bitcast.13, ...), custom_call_target="tpu_custom_call" | custom-call | tf_op jit(solution)/shard_map/step/pallas_call | solution.py:465
  76.0 1.4 %copy.18 = f32[8,8,128]{2,1,0:T(8,128)} copy(f32[8,8,128]{2,1,0:T(8,128)} %bitcast.18) | data formatting | bytes 65536
  77.4 1.4 %copy.19 = f32[8,8,128]{2,1,0:T(8,128)} copy(f32[8,8,128]{2,1,0:T(8,128)} %bitcast.17) | data formatting | bytes 65536
  78.8 0.0 copy-start
  78.8 3.1 %copy.20 = f32[32,16384]{1,0:T(8,128)} copy(f32[32,16384]{1,0:T(8,128)} %get-tuple-element.18) | data formatting | bytes 4194304
  81.9 0.0 copy-done
  81.9 0.6 copy.21
Async XLA Ops:
  78.8 3.1 %copy-start = (f32[32,4,128]{2,1,0:T(4,128)S(1)}, f32[32,4,128]{2,1,0:T(4,128)}, u32[]{:S(2)}) copy-start(f32[32,4,128]{2,1,0:T(4,128)} %get-tuple-element.11) | copy-start | bytes 196612

commit v2 on v1

--- a/solution.py
+++ b/solution.py
@@ -13,14 +13,12 @@
 f32 = jnp.float32
 bf16 = jnp.bfloat16
 i32 = jnp.int32
-HIGH = lax.Precision.HIGHEST
 
 N = 32
 NG = 4
 PD = 8192
 CH = PD // 128
 CAP = 512
-COLS = 64
 
 _GROUPS = [
     [(2, 2)],
@@ -30,7 +28,10 @@
     [(0, 2), (2, 0)],
     [(0, 1), (0, 3), (1, 0), (3, 0)],
 ]
-_ORDER = [(a, b, c) for g in _GROUPS for c in (0, 1) for (a, b) in g] + [(0, 0, 1)]
+_ORDER = [(a, b, c) for g in _GROUPS for c in (0, 1) for (a, b) in g] + [
+    (0, 0, 1),
+    (0, 0, 0),
+]
 _CODES = [a * 8 + b * 2 + c for (a, b, c) in _ORDER]
 _WORDS = [
     sum(code << (5 * j) for j, code in enumerate(_CODES[6 * w : 6 * w + 6]))
@@ -82,13 +83,13 @@
 
 
 def kernel(
-    vel_in, vrow_in, scal_in, mass_in, pw_in, cell_in, mig_in, part, rmat_in, enth_in,
+    vel_in, vmap_in, scal_in, mass_in, pw_in, cell_in, mig_in, part, rmat_in, enth_in,
     ce, cd, ms, mm,
-    vel, vrow, scal, mass, pw, cell, mig, rmat, enth,
+    vel, vmap, scal, mass, pw, cell, mig, rmat, enth,
     hx, hy, ysnd, ypad, q2, q2t, wmat, possend, posrecv, fsend, frecv, bsend, brecv,
-    rows, pt, gbuf, slot, srcv, mbuf, tab, frac, kinp, en, sendbuf,
-    part_s, src_s,
-    isem, lsem, hss, hrs, pss, prs, css, crs, mss, mrs, dss, drs, bss, brs,
+    rows, pt, gbuf, slot, srcv, partv, iacc, bacc, mbuf, tab, frac, kinp, sendbuf,
+    idx_s,
+    isem, lsem, xsem, hss, hrs, pss, prs, css, crs, mss, mrs, dss, drs, bss, brs,
 ):
     me = lax.axis_index("flow")
     g = lax.axis_index("grp")
@@ -100,8 +101,8 @@
         pltpu.make_async_copy(src, dst, isem.at[k])
         for k, (src, dst) in enumerate(
             [
-                (vrow_in, vrow), (vel_in, vel), (scal_in, scal), (mig_in, mig), (mass_in, mass),
-                (pw_in, pw), (cell_in, cell), (rmat_in, rmat), (enth_in, enth), (part, part_s),
+                (vmap_in, vmap), (vel_in, vel), (scal_in, scal), (mig_in, mig), (mass_in, mass),
+                (pw_in, pw), (cell_in, cell), (rmat_in, rmat), (enth_in, enth), (part, partv),
             ]
         )
     ]
@@ -126,11 +127,19 @@
         )
     loads[0].wait()
 
-    v = vrow[0:1, :]
     lane1 = iota((1, 128), 1)
     field = jnp.right_shift(lane1, 6)
-    target = jnp.right_shift(v, 6)
-    place = jnp.bitwise_and(v, 63) + 64 * field
+    spread = jnp.where(
+        jnp.bitwise_and(iota((8, 128), 1), 7) == iota((8, 128), 0), 1.0, 0.0
+    )
+    own_row = jnp.bitwise_and(jnp.right_shift(iota((8, 128), 1), 3), 7) == iota((8, 128), 0)
+
+    def as_row(x):
+        wide = jnp.dot(x.astype(f32), spread, preferred_element_type=f32)
+        return jnp.sum(jnp.where(own_row, wide, 0.0), axis=0, keepdims=True).astype(i32)
+
+    target = as_row(jnp.right_shift(vmap[...], 6))
+    place = as_row(jnp.bitwise_and(vmap[...], 63)) + 64 * field
     key = jnp.broadcast_to((target + 64 * field).astype(f32), (128, 128))
     earlier = jnp.where(
         jnp.logical_and(key.T == key, iota((128, 128), 0) < iota((128, 128), 1)), 1.0, 0.0
@@ -152,6 +161,15 @@
             ysnd[0, c, x : x + 1, :] = vel[c, x, 0:1, :]
             ysnd[1, c, x : x + 1, :] = vel[c, x, 7:8, :]
 
+    def to_rows(c, _):
+        col = pl.ds(pl.multiple_of(c * 128, 128), 128)
+        x = scal[:, col]
+        rows[col, :] = jnp.concatenate([x, x, x, x], axis=0).T
+        return 0
+
+    loads[2].wait()
+    lax.fori_loop(0, CH, to_rows, 0, unroll=8)
+
     pl.semaphore_wait(barrier, N - 1 + 2)
 
     nxt, prv = lax.rem(me + 1, N), lax.rem(me + N - 1, N)
@@ -190,15 +208,36 @@
 
     exchange(possend, posrecv, pss, prs, lsem.at[1])
 
-    loads[2].wait()
-
-    def to_rows(c, _):
-        col = pl.ds(pl.multiple_of(c * 128, 128), 128)
-        x = scal[:, col]
-        rows[col, :] = jnp.concatenate([x, x, x, x], axis=0).T
-        return 0
-
-    lax.fori_loop(0, CH // 2, to_rows, 0, unroll=8)
+    for copy in loads[3:9]:
+        copy.wait()
+
+    tri = jnp.concatenate(
+        [
+            jnp.where(iota((128, 128), 0) < iota((128, 128), 1), 1.0, 0.0).astype(bf16),
+            jnp.ones((128, 128), bf16),
+        ],
+        axis=1,
+    )
+
+    def ranks(b, carry):
+        hots = []
+        for j in range(8):
+            p = mig[pl.ds(b * 8 + j, 1), :]
+            hots.append(jnp.where(iota((32, 128), 0) == p, 1.0, 0.0))
+        hot = jnp.concatenate(hots, axis=0)
+        pre = dot(hot.astype(bf16), tri)
+        out = []
+        for j in range(8):
+            sl = slice(32 * j, 32 * j + 32)
+            out.append(
+                jnp.sum(hots[j] * (pre[sl, :128] + carry), axis=0, keepdims=True).astype(i32)
+            )
+            carry = carry + pre[sl, 128:]
+        r8 = pl.ds(pl.multiple_of(b * 8, 8), 8)
+        slot[r8, :] = mig[r8, :] * CAP + jnp.concatenate(out, axis=0)
+        return carry
+
+    lax.fori_loop(0, 8, ranks, jnp.zeros((32, 128), f32))
 
     for copy in halo:
         copy.wait()
@@ -232,40 +271,7 @@
     fsend[...] = select_dot(q2[...], both)
     exchange(fsend, frecv, css, crs, lsem.at[2])
 
-    lax.fori_loop(CH // 2, CH, to_rows, 0, unroll=8)
-
-    for copy in loads[3:9]:
-        copy.wait()
-
-    tri = jnp.concatenate(
-        [
-            jnp.where(iota((128, 128), 0) < iota((128, 128), 1), 1.0, 0.0).astype(bf16),
-            jnp.ones((128, 128), bf16),
-        ],
-        axis=1,
-    )
-
-    def ranks(b, carry):
-        hots = []
-        for j in range(8):
-            p = mig[pl.ds(b * 8 + j, 1), :]
-            hots.append(jnp.where(iota((32, 128), 0) == p, 1.0, 0.0))
-        hot = jnp.concatenate(hots, axis=0)
-        pre = dot(hot.astype(bf16), tri)
-        out = []
-        for j in range(8):
-            sl = slice(32 * j, 32 * j + 32)
-            out.append(
-                jnp.sum(hots[j] * (pre[sl, :128] + carry), axis=0, keepdims=True).astype(i32)
-            )
-            carry = carry + pre[sl, 128:]
-        r8 = pl.ds(pl.multiple_of(b * 8, 8), 8)
-        slot[r8, :] = mig[r8, :] * CAP + jnp.concatenate(out, axis=0)
-        return carry
-
-    lax.fori_loop(0, 8, ranks, jnp.zeros((32, 128), f32))
-
-    def inverse(b, acc):
+    def inverse(b):
         left, right = [], []
         sub = iota((128, 128), 0)
         for j in range(4):
@@ -284,35 +290,50 @@
                     [jnp.where(at, w, 0.0).astype(bf16) for w in (hi, lo, m_hi, m_lo)], axis=0
                 )
             )
-        return acc + dot_nt(jnp.concatenate(left, axis=1), jnp.concatenate(right, axis=1))
-
-    inv = lax.fori_loop(0, CH // 4, inverse, jnp.zeros((128, 512), f32))
-    srcv[...] = jnp.clip((PD - (inv[:, 0:128] * 128.0 + inv[:, 128:256])).astype(i32), 0, PD)
+        iacc[...] += dot_nt(jnp.concatenate(left, axis=1), jnp.concatenate(right, axis=1))
+
+    lanes = iota((1, 128), 1)
+    quarter = [lanes < 32, lanes < 64, lanes < 96]
+
+    def fetch(src, k):
+        return pltpu.make_async_copy(src, idx_s.at[k], xsem.at[k])
+
+    def gather(k):
+        for r in range(128):
+            a, b, c, d = [rows[pl.ds(idx_s[k, q, r], 1), :] for q in range(4)]
+            gbuf[k, r : r + 1, :] = jnp.where(
+                quarter[1], jnp.where(quarter[0], a, b), jnp.where(quarter[2], c, d)
+            )
+        return gbuf[k].T
+
+    loads[9].wait()
+    for k in range(2):
+        fetch(partv.at[k], k).start()
+    iacc[...] = jnp.zeros((128, 512), f32)
+    bacc[...] = jnp.zeros((64, 512), f32)
+
+    def partners(i, _):
+        for k in range(2):
+            b = 2 * i + k
+            fetch(partv.at[b], k).wait()
+            t = gather(k)
+            fetch(partv.at[jnp.minimum(b + 2, 14 + k)], k).start()
+            for q in range(4):
+                col = pl.ds(pl.multiple_of(b * 512 + q * 128, 128), 128)
+                pt[:, col] = t[32 * q : 32 * q + 32, :]
+            inverse(b)
+        return 0
+
+    lax.fori_loop(0, 8, partners, 0)
+    for k in range(2):
+        fetch(partv.at[14 + k], k).wait()
+
+    inv = iacc[...]
+    source = jnp.clip((PD - (inv[:, 0:128] * 128.0 + inv[:, 128:256])).astype(i32), 0, PD)
     moved = inv[:, 256:384] + inv[:, 384:512]
     for p in range(N):
+        srcv[p] = source[4 * p : 4 * p + 4, :]
         mbuf[p] = moved[4 * p : 4 * p + 4, :]
-    loads[9].wait()
-
-    lanes = iota((1, 128), 1)
-    quarter = [lanes < 32, lanes < 64, lanes < 96]
-
-    def packed(index):
-        a, b, c, d = [rows[pl.ds(index(q), 1), :] for q in range(4)]
-        return jnp.where(quarter[1], jnp.where(quarter[0], a, b), jnp.where(quarter[2], c, d))
-
-    def partners(b, _):
-        for r in range(128):
-            gbuf[r : r + 1, :] = packed(lambda q: part_s[4 * b + q, r])
-        t = gbuf[...].T
-        for q in range(4):
-            col = pl.ds(pl.multiple_of(b * 512 + q * 128, 128), 128)
-            pt[:, col] = t[32 * q : 32 * q + 32, :]
-        return 0
-
-    lax.fori_loop(0, 16, partners, 0)
-
-    src_copy = pltpu.make_async_copy(srcv, src_s, lsem.at[3])
-    src_copy.start()
 
     def send_mass(t, _):
         p = peer(t)
@@ -349,8 +370,15 @@
         frac[sl, :] = 1.0 - jnp.exp(-mix_step * pw[sl, :] * found[2 * k])
         kinp[sl, :] = found[2 * k + 1]
 
-    rates = rmat[...]
-    forms = jnp.broadcast_to(enth[...], (8, 32))
+    for k in range(2):
+        fetch(srcv.at[ordered_peer(k, me)], k).start()
+
+    r_hi = rmat[...].astype(bf16)
+    r_lo = (rmat[...] - r_hi.astype(f32)).astype(bf16)
+    rates = jnp.concatenate([r_hi, r_hi, r_lo], axis=1)
+    f_hi = jnp.broadcast_to(enth[...], (8, 32)).astype(bf16)
+    f_lo = (jnp.broadcast_to(enth[...], (8, 32)) - f_hi.astype(f32)).astype(bf16)
+    forms = jnp.concatenate([f_hi, f_hi, f_lo], axis=1)
 
     def react(b, _):
         mixed = []
@@ -360,51 +388,36 @@
             s = scal[:, col]
             mixed.append(s + frac[pl.ds(c, 1), :] * (pt[:, col] - s))
         mixed = jnp.concatenate(mixed, axis=1)
-        rate = jnp.dot(rates, mixed, precision=HIGH, preferred_element_type=f32)
-        out = mixed + react_step * jnp.tanh(rate)
-        e = jnp.dot(forms, out, precision=HIGH, preferred_element_type=f32)
+        hi, lo = split2(mixed)
+        out = mixed + react_step * jnp.tanh(dot(rates, jnp.concatenate([hi, lo, hi], axis=0)))
+        pt[:, pl.ds(pl.multiple_of(b * 512, 512), 512)] = out
         for j in range(4):
-            c = b * 4 + j
-            en[pl.ds(c, 1), :] = e[0:1, 128 * j : 128 * j + 128] + kinp[pl.ds(c, 1), :]
             x = out[:, 128 * j : 128 * j + 128]
-            col = pl.ds(pl.multiple_of(c * 128, 128), 128)
+            col = pl.ds(pl.multiple_of(b * 512 + j * 128, 128), 128)
             rows[col, :] = jnp.concatenate([x, x, x, x], axis=0).T
         return 0
 
-    lax.fori_loop(0, 16, react, 0)
+    lax.fori_loop(0, 16, react, 0, unroll=2)
     rows[PD : PD + 8, :] = jnp.zeros((8, 128), f32)
-    src_copy.wait()
 
     def slots(d):
         return ms.at[:, pl.ds(pl.multiple_of(d * CAP, CAP), CAP)]
 
-    def gather_block(p):
-        for r in range(128):
-            gbuf[r : r + 1, :] = packed(lambda q: src_s[4 * p + q, r])
-        t = gbuf[...].T
-        for q in range(4):
-            sendbuf[p, :, 128 * q : 128 * q + 128] = t[32 * q : 32 * q + 32, :]
-
     def data(p, d):
         return remote(sendbuf.at[p], slots(d), dss.at[p], drs.at[d], (p, g))
 
-    def send_data(t, _):
-        p = ordered_peer(t, me)
-        gather_block(p)
-        remote(sendbuf.at[p], slots(me), dss.at[p], drs.at[me], (p, g)).start()
-        return 0
-
-    lax.fori_loop(0, 16, send_data, 0)
-
-    def bins(b, acc):
+    def bins(b):
         left, right = [], []
         sub = iota((128, 128), 0)
         sub64 = iota((64, 128), 0)
+        out = pt[:, pl.ds(pl.multiple_of(b * 512, 512), 512)]
+        hi, lo = split2(out)
+        es = dot(forms, jnp.concatenate([hi, lo, hi], axis=0))
         for j in range(4):
             c = b * 4 + j
             w = cell[pl.ds(c, 1), :]
             m = mass[pl.ds(c, 1), :]
-            e = m * en[pl.ds(c, 1), :]
+            e = m * (es[0:1, 128 * j : 128 * j + 128] + kinp[pl.ds(c, 1), :])
             m_hi = m.astype(bf16).astype(f32)
             e_hi = e.astype(bf16).astype(f32)
             left.append(jnp.where(sub64 == jnp.right_shift(w, 7), 1.0, 0.0).astype(bf16))
@@ -418,17 +431,36 @@
                     axis=0,
                 )
             )
-        return acc + dot_nt(jnp.concatenate(left, axis=1), jnp.concatenate(right, axis=1))
-
-    sums = lax.fori_loop(0, CH // 4, bins, jnp.zeros((64, 512), f32))
+        bacc[...] += dot_nt(jnp.concatenate(left, axis=1), jnp.concatenate(right, axis=1))
+
+    def send_pair(i, with_bins):
+        for k in range(2):
+            t = 2 * i + k
+            p = ordered_peer(t, me)
+            fetch(srcv.at[p], k).wait()
+            block = gather(k)
+            fetch(srcv.at[ordered_peer(jnp.minimum(t + 2, 30 + k), me)], k).start()
+            for q in range(4):
+                sendbuf[p, :, 128 * q : 128 * q + 128] = block[32 * q : 32 * q + 32, :]
+            if with_bins:
+                bins(t)
+
+            @pl.when(t < N - 1)
+            def _():
+                remote(sendbuf.at[p], slots(me), dss.at[p], drs.at[me], (p, g)).start()
+
+        return 0
+
+    lax.fori_loop(0, 8, lambda i, _: send_pair(i, True), 0)
+    sums = bacc[...]
     table = jnp.concatenate(
         [sums[:, 0:128] + sums[:, 128:256], sums[:, 256:384] + sums[:, 384:512]], axis=0
     )
     bsend[...] = select_dot(wmat[...], table)
     exchange(bsend, brecv, bss, brs, lsem.at[1])
-
-    lax.fori_loop(16, N - 1, send_data, 0)
-    gather_block(me)
+    lax.fori_loop(8, 16, lambda i, _: send_pair(i, False), 0)
+    for k in range(2):
+        fetch(srcv.at[ordered_peer(30 + k, me)], k).wait()
     own = pltpu.make_async_copy(sendbuf.at[me], slots(me), lsem.at[5])
     own.start()
 
@@ -452,14 +484,22 @@
     own.wait()
 
 
+def write_out(*refs):
+    sems = refs[8]
+    copies = [pltpu.make_async_copy(refs[k], refs[k + 4], sems.at[k]) for k in (2, 3, 0, 1)]
+    for copy in copies:
+        copy.start()
+    for copy in copies:
+        copy.wait()
+
+
 def per_device(
     velocity, column_slot, scalars, mass, pair_weight, particle_cell, mix_partner, migrate_to,
     rate_matrix, enthalpy,
 ):
-    slots = column_slot.reshape(1, COLS)
-    vrow = jnp.broadcast_to(jnp.concatenate([slots, slots], axis=1), (8, 128))
     vmem = pl.BlockSpec(memory_space=pltpu.VMEM)
-    hbm = pl.BlockSpec(memory_space=pl.ANY)
+    hbm = pl.BlockSpec(memory_space=pltpu.HBM)
+    anywhere = pl.BlockSpec(memory_space=pl.ANY)
     V = pltpu.VMEM
     D = pltpu.SemaphoreType.DMA
     ce, cd, ms, mm = pl.pallas_call(
@@ -471,10 +511,10 @@
             jax.ShapeDtypeStruct((N, 4, 128), f32),
         ),
         in_specs=[hbm] * 10,
-        out_specs=(vmem, vmem, hbm, hbm),
+        out_specs=(vmem, vmem, vmem, vmem),
         scratch_shapes=[
             V((3, 8, 8, 128), f32),
-            V((8, 128), i32),
+            V((8, 8), i32),
             V((32, PD), f32),
             V((CH, 128), f32),
             V((CH, 128), f32),
@@ -497,19 +537,21 @@
             V((256, 128), f32),
             V((PD + 8, 128), f32),
             V((32, PD), f32),
-            V((128, 128), f32),
+            V((2, 128, 128), f32),
             V((CH, 128), i32),
-            V((128, 128), i32),
+            V((N, 4, 128), i32),
+            V((16, 4, 128), i32),
+            V((128, 512), f32),
+            V((64, 512), f32),
             V((N, 4, 128), f32),
             V((128, 128), f32),
             V((CH, 128), f32),
             V((CH, 128), f32),
-            V((CH, 128), f32),
             V((N, 32, CAP), f32),
-            pltpu.SMEM((CH, 128), i32),
-            pltpu.SMEM((128, 128), i32),
+            pltpu.SMEM((2, 4, 128), i32),
             D((10,)),
             D((6,)),
+            D((2,)),
             D((4,)), D((4,)),
             D((N,)), D((N,)),
             D((N,)), D((N,)),
@@ -518,21 +560,40 @@
             D((N,)), D((N,)),
         ],
         compiler_params=pltpu.CompilerParams(
-            collective_id=0, has_side_effects=True, vmem_limit_bytes=60 << 20
+            collective_id=0, has_side_effects=True, vmem_limit_bytes=24 << 20
         ),
         name="step",
     )(
-        velocity,
-        vrow,
-        scalars,
-        mass.reshape(CH, 128),
-        pair_weight.reshape(CH, 128),
-        particle_cell.reshape(CH, 128),
-        migrate_to.reshape(CH, 128),
-        mix_partner.reshape(CH, 128),
-        rate_matrix,
-        enthalpy.reshape(1, 32),
+        *[
+            pltpu.with_memory_space_constraint(x, pltpu.HBM)
+            for x in (
+                velocity,
+                column_slot,
+                scalars,
+                mass.reshape(CH, 128),
+                pair_weight.reshape(CH, 128),
+                particle_cell.reshape(CH, 128),
+                migrate_to.reshape(CH, 128),
+                mix_partner.reshape(16, 4, 128),
+                rate_matrix,
+                enthalpy.reshape(1, 32),
+            )
+        ]
     )
+    ce, cd, ms, mm = pl.pallas_call(
+        write_out,
+        out_shape=(
+            jax.ShapeDtypeStruct((64, 128), f32),
+            jax.ShapeDtypeStruct((64, 128), f32),
+            jax.ShapeDtypeStruct((32, N * CAP), f32),
+            jax.ShapeDtypeStruct((N, 4, 128), f32),
+        ),
+        in_specs=[vmem] * 4,
+        out_specs=(hbm,) * 4,
+        scratch_shapes=[D((4,))],
+        compiler_params=pltpu.CompilerParams(vmem_limit_bytes=16 << 20),
+        name="write_out",
+    )(ce, cd, ms, mm)
     return (ce.reshape(8, 8, 128), cd.reshape(8, 8, 128), ms, mm.reshape(N * CAP))
 
 

time: 82.8 us -> 66.8 us (0.81)
  Pallas kernels: 74 us -> 66 us
  local copies, waits for them, and re-layouts: 7.83 us -> 0 us
    pallas_call x1, Pallas kernels: 74 us -> 64.7 us  [per_device(): pl.pallas_call(kernel, out_shape=(jax.ShapeDtypeStruct((64, 128), f32), j...]
    unnamed x6 -> x0, local copies, waits for them, and re-layouts: 6.46 us -> none
    pallas_call x0 -> x1, Pallas kernels: none -> 1.37 us  [per_device(): pl.pallas_call(write_out, out_shape=(jax.ShapeDtypeStruct((64, 128), f32)...]
where the time goes in v2:
time: 66.8 us; the launch traced here: 66.7 us
  Pallas kernels  66 us (99%)
    pallas_call x1, Pallas kernels, per_device(): pl.pallas_call(kernel, out_shape=(jax.ShapeDtypeStruct((64, 128), f32), j...  64.7 us
    pallas_call x1, Pallas kernels, per_device(): pl.pallas_call(write_out, out_shape=(jax.ShapeDtypeStruct((64, 128), f32)...  1.37 us

profile of v2, /device:TPU:1, one launch (start us, length us, event | category | flops | bytes accessed | tf_op | source)
XLA Modules:
  0.0 66.7 jit_solution(4643065099873670115)
XLA Ops:
  0.6 64.7 %step.1 = (f32[64,128]{1,0:T(8,128)S(1)}, f32[64,128]{1,0:T(8,128)S(1)}, f32[32,16384]{1,0:T(8,128)S(1)}, f32[32,4,128]{2,1,0:T(4,128)S(1)}) custom-call(f32[3,8,8,128]{3,2,1,0:T(8,128)} %vel_in.1, s32[8,8]{1,0:T(8,128)} %vmap_in.1, f32[32,8192]{1,0:T(8,128)} %scal_in.1, f32[64,128]{1,0:T(8,128)} %bitcast.9, f32[64,128]{1,0:T(8,128)} %bitcast.10, ...), custom_call_target="tpu_custom_call" | custom-call | tf_op jit(solution)/shard_map/step/pallas_call | solution.py:505
  65.3 1.4 %write_out.1 = (f32[64,128]{1,0:T(8,128)}, f32[64,128]{1,0:T(8,128)}, f32[32,16384]{1,0:T(8,128)}, f32[32,4,128]{2,1,0:T(4,128)}) custom-call(f32[64,128]{1,0:T(8,128)S(1)} %get-tuple-element.12.refs_0_, f32[64,128]{1,0:T(8,128)S(1)} %get-tuple-element.13.refs_1_, f32[32,16384]{1,0:T(8,128)S(1)} %get-tuple-element.14.refs_2_, ...), custom_call_target="tpu_custom_call" | custom-call | tf_op jit(solution)/shard_map/write_out/pallas_call | solution.py:583

commit v3 on v2

--- a/solution.py
+++ b/solution.py
@@ -87,7 +87,7 @@
     ce, cd, ms, mm,
     vel, vmap, scal, mass, pw, cell, mig, rmat, enth,
     hx, hy, ysnd, ypad, q2, q2t, wmat, possend, posrecv, fsend, frecv, bsend, brecv,
-    rows, pt, gbuf, slot, srcv, partv, iacc, bacc, mbuf, tab, frac, kinp, sendbuf,
+    rows, pt, gbuf, slot, srcv, partv, iacc, bacc, mbuf, tab, frac, found, sendbuf,
     idx_s,
     isem, lsem, xsem, hss, hrs, pss, prs, css, crs, mss, mrs, dss, drs, bss, brs,
 ):
@@ -161,15 +161,6 @@
             ysnd[0, c, x : x + 1, :] = vel[c, x, 0:1, :]
             ysnd[1, c, x : x + 1, :] = vel[c, x, 7:8, :]
 
-    def to_rows(c, _):
-        col = pl.ds(pl.multiple_of(c * 128, 128), 128)
-        x = scal[:, col]
-        rows[col, :] = jnp.concatenate([x, x, x, x], axis=0).T
-        return 0
-
-    loads[2].wait()
-    lax.fori_loop(0, CH, to_rows, 0, unroll=8)
-
     pl.semaphore_wait(barrier, N - 1 + 2)
 
     nxt, prv = lax.rem(me + 1, N), lax.rem(me + N - 1, N)
@@ -208,7 +199,7 @@
 
     exchange(possend, posrecv, pss, prs, lsem.at[1])
 
-    for copy in loads[3:9]:
+    for copy in loads[2:]:
         copy.wait()
 
     tri = jnp.concatenate(
@@ -222,6 +213,9 @@
     def ranks(b, carry):
         hots = []
         for j in range(8):
+            col = pl.ds(pl.multiple_of((b * 8 + j) * 128, 128), 128)
+            x = scal[:, col]
+            rows[col, :] = jnp.concatenate([x, x, x, x], axis=0).T
             p = mig[pl.ds(b * 8 + j, 1), :]
             hots.append(jnp.where(iota((32, 128), 0) == p, 1.0, 0.0))
         hot = jnp.concatenate(hots, axis=0)
@@ -304,29 +298,58 @@
             gbuf[k, r : r + 1, :] = jnp.where(
                 quarter[1], jnp.where(quarter[0], a, b), jnp.where(quarter[2], c, d)
             )
-        return gbuf[k].T
-
-    loads[9].wait()
+
     for k in range(2):
         fetch(partv.at[k], k).start()
     iacc[...] = jnp.zeros((128, 512), f32)
     bacc[...] = jnp.zeros((64, 512), f32)
 
-    def partners(i, _):
+    def put_partners(b, t):
+        for q in range(4):
+            col = pl.ds(pl.multiple_of(b * 512 + q * 128, 128), 128)
+            pt[:, col] = t[32 * q : 32 * q + 32, :]
+
+    def lookup(n0):
+        acc = [found[8 * k : 8 * k + 8, :] for k in range(16)]
+        for j in range(8):
+            om = jnp.broadcast_to(tab[pl.ds(n0 + j, 1), :], (8, 128))
+            ki = jnp.broadcast_to(tab[pl.ds(n0 + j + 64, 1), :], (8, 128))
+            for k in range(8):
+                w = cell[8 * k : 8 * k + 8, :]
+                z = jnp.bitwise_and(w, 127)
+                here = jnp.right_shift(w, 7) == n0 + j
+                acc[k] = jnp.where(here, jnp.take_along_axis(om, z, axis=1), acc[k])
+                acc[8 + k] = jnp.where(here, jnp.take_along_axis(ki, z, axis=1), acc[8 + k])
+        for k in range(16):
+            found[8 * k : 8 * k + 8, :] = acc[k]
+
+    def partners(i, with_lookup):
         for k in range(2):
             b = 2 * i + k
             fetch(partv.at[b], k).wait()
-            t = gather(k)
+            before = gbuf[1 - k].T
+            gather(k)
+            put_partners(jnp.maximum(b - 1, 0), before)
+            inverse(b)
+            if with_lookup:
+                lookup(8 * (b - 8))
             fetch(partv.at[jnp.minimum(b + 2, 14 + k)], k).start()
-            for q in range(4):
-                col = pl.ds(pl.multiple_of(b * 512 + q * 128, 128), 128)
-                pt[:, col] = t[32 * q : 32 * q + 32, :]
-            inverse(b)
         return 0
 
-    lax.fori_loop(0, 8, partners, 0)
+    lax.fori_loop(0, 4, lambda i, _: partners(i, False), 0)
+
+    arrive(possend, posrecv, pss, prs, lsem.at[1])
+    pos = posrecv[...]
+    wmat[...] = jnp.where(pos == iota((256, 128), 1).astype(f32), 1.0, 0.0).astype(bf16)
+    wt = jnp.where(pos.T == iota((128, 256), 0).astype(f32), 1.0, 0.0).astype(bf16)
+    arrive(fsend, frecv, css, crs, lsem.at[2])
+    tab[...] = select_dot(wt, frecv[...])
+    found[...] = jnp.zeros((128, 128), f32)
+
+    lax.fori_loop(4, 8, lambda i, _: partners(i, True), 0)
     for k in range(2):
         fetch(partv.at[14 + k], k).wait()
+    put_partners(15, gbuf[1].T)
 
     inv = iacc[...]
     source = jnp.clip((PD - (inv[:, 0:128] * 128.0 + inv[:, 128:256])).astype(i32), 0, PD)
@@ -344,31 +367,7 @@
     own_mass = pltpu.make_async_copy(mbuf.at[me], mm.at[me], lsem.at[4])
     own_mass.start()
 
-    arrive(possend, posrecv, pss, prs, lsem.at[1])
-    pos = posrecv[...]
-    wmat[...] = jnp.where(pos == iota((256, 128), 1).astype(f32), 1.0, 0.0).astype(bf16)
-    wt = jnp.where(pos.T == iota((128, 256), 0).astype(f32), 1.0, 0.0).astype(bf16)
-    arrive(fsend, frecv, css, crs, lsem.at[2])
-    tab[...] = select_dot(wt, frecv[...])
-
-    cz = [jnp.bitwise_and(cell[8 * k : 8 * k + 8, :], 127) for k in range(8)]
-    cp = [jnp.right_shift(cell[8 * k : 8 * k + 8, :], 7) for k in range(8)]
-
-    def lookup(n, acc):
-        om = jnp.broadcast_to(tab[pl.ds(n, 1), :], (8, 128))
-        ki = jnp.broadcast_to(tab[pl.ds(n + 64, 1), :], (8, 128))
-        out = []
-        for k in range(8):
-            here = cp[k] == n
-            out.append(jnp.where(here, jnp.take_along_axis(om, cz[k], axis=1), acc[2 * k]))
-            out.append(jnp.where(here, jnp.take_along_axis(ki, cz[k], axis=1), acc[2 * k + 1]))
-        return tuple(out)
-
-    found = lax.fori_loop(0, 64, lookup, tuple(jnp.zeros((8, 128), f32) for _ in range(16)))
-    for k in range(8):
-        sl = slice(8 * k, 8 * k + 8)
-        frac[sl, :] = 1.0 - jnp.exp(-mix_step * pw[sl, :] * found[2 * k])
-        kinp[sl, :] = found[2 * k + 1]
+    frac[...] = 1.0 - jnp.exp(-mix_step * pw[...] * found[0:64, :])
 
     for k in range(2):
         fetch(srcv.at[ordered_peer(k, me)], k).start()
@@ -417,7 +416,7 @@
             c = b * 4 + j
             w = cell[pl.ds(c, 1), :]
             m = mass[pl.ds(c, 1), :]
-            e = m * (es[0:1, 128 * j : 128 * j + 128] + kinp[pl.ds(c, 1), :])
+            e = m * (es[0:1, 128 * j : 128 * j + 128] + found[pl.ds(64 + c, 1), :])
             m_hi = m.astype(bf16).astype(f32)
             e_hi = e.astype(bf16).astype(f32)
             left.append(jnp.where(sub64 == jnp.right_shift(w, 7), 1.0, 0.0).astype(bf16))
@@ -433,37 +432,54 @@
             )
         bacc[...] += dot_nt(jnp.concatenate(left, axis=1), jnp.concatenate(right, axis=1))
 
-    def send_pair(i, with_bins):
+    def put_block(p, t):
+        for q in range(4):
+            sendbuf[p, :, 128 * q : 128 * q + 128] = t[32 * q : 32 * q + 32, :]
+
+    def send_pair(i, peers, with_bins):
+        last, now, soon = peers
         for k in range(2):
             t = 2 * i + k
-            p = ordered_peer(t, me)
-            fetch(srcv.at[p], k).wait()
-            block = gather(k)
-            fetch(srcv.at[ordered_peer(jnp.minimum(t + 2, 30 + k), me)], k).start()
-            for q in range(4):
-                sendbuf[p, :, 128 * q : 128 * q + 128] = block[32 * q : 32 * q + 32, :]
+            fetch(srcv.at[now], k).wait()
+            later = ordered_peer(jnp.minimum(t + 2, N - 1), me)
+            before = gbuf[1 - k].T
+            gather(k)
+            put_block(last, before)
             if with_bins:
                 bins(t)
-
-            @pl.when(t < N - 1)
-            def _():
-                remote(sendbuf.at[p], slots(me), dss.at[p], drs.at[me], (p, g)).start()
-
-        return 0
-
-    lax.fori_loop(0, 8, lambda i, _: send_pair(i, True), 0)
+            fetch(srcv.at[later], k).start()
+
+            @pl.when(t > 0)
+            def _(last=last):
+                remote(sendbuf.at[last], slots(me), dss.at[last], drs.at[me], (last, g)).start()
+
+            last, now, soon = now, soon, later
+        return last, now, soon
+
+    first, second = ordered_peer(0, me), ordered_peer(1, me)
+    peers = lax.fori_loop(0, 8, lambda i, c: send_pair(i, c, True), (first, first, second))
     sums = bacc[...]
     table = jnp.concatenate(
         [sums[:, 0:128] + sums[:, 128:256], sums[:, 256:384] + sums[:, 384:512]], axis=0
     )
     bsend[...] = select_dot(wmat[...], table)
     exchange(bsend, brecv, bss, brs, lsem.at[1])
-    lax.fori_loop(8, 16, lambda i, _: send_pair(i, False), 0)
+    lax.fori_loop(8, 16, lambda i, c: send_pair(i, c, False), peers)
     for k in range(2):
-        fetch(srcv.at[ordered_peer(30 + k, me)], k).wait()
+        fetch(srcv.at[me], k).wait()
+    put_block(me, gbuf[1].T)
     own = pltpu.make_async_copy(sendbuf.at[me], slots(me), lsem.at[5])
     own.start()
 
+    def masses(t, _):
+        p = peer(t)
+        copy = remote(mbuf.at[p], mm.at[p], mss.at[p], mrs.at[p], (p, g))
+        copy.wait_send()
+        copy.wait_recv()
+        return 0
+
+    lax.fori_loop(1, N, masses, 0)
+    own_mass.wait()
     arrive(bsend, brecv, bss, brs, lsem.at[1])
     back = select_dot(q2t[...], brecv[...])
     ce[...] = back[0:64, :]
@@ -471,16 +487,12 @@
 
     def finish(t, _):
         p = peer(t)
-        copy = remote(mbuf.at[p], mm.at[p], mss.at[p], mrs.at[p], (p, g))
-        copy.wait_send()
-        copy.wait_recv()
         copy = data(p, p)
         copy.wait_send()
         copy.wait_recv()
         return 0
 
     lax.fori_loop(1, N, finish, 0)
-    own_mass.wait()
     own.wait()
 
 
@@ -546,7 +558,7 @@
             V((N, 4, 128), f32),
             V((128, 128), f32),
             V((CH, 128), f32),
-            V((CH, 128), f32),
+            V((128, 128), f32),
             V((N, 32, CAP), f32),
             pltpu.SMEM((2, 4, 128), i32),
             D((10,)),

time: 66.8 us -> 62.5 us (0.936)
  Pallas kernels: 66 us -> 61.7 us
    pallas_call x1, Pallas kernels: 64.7 us -> 60.3 us  [per_device(): pl.pallas_call(kernel, out_shape=(jax.ShapeDtypeStruct((64, 128), f32), j...]
where the time goes in v3:
time: 62.5 us; the launch traced here: 62.3 us
  Pallas kernels  61.7 us (99%)
  between operations  0.64 us (1%)
    pallas_call x1, Pallas kernels, per_device(): pl.pallas_call(kernel, out_shape=(jax.ShapeDtypeStruct((64, 128), f32), j...  60.3 us
    pallas_call x1, Pallas kernels, per_device(): pl.pallas_call(write_out, out_shape=(jax.ShapeDtypeStruct((64, 128), f32)...  1.37 us

profile of v3, /device:TPU:1, one launch (start us, length us, event | category | flops | bytes accessed | tf_op | source)
XLA Modules:
  0.0 62.3 jit_solution(6575420421042238984)
XLA Ops:
  0.6 60.3 %step.1 = (f32[64,128]{1,0:T(8,128)S(1)}, f32[64,128]{1,0:T(8,128)S(1)}, f32[32,16384]{1,0:T(8,128)S(1)}, f32[32,4,128]{2,1,0:T(4,128)S(1)}) custom-call(f32[3,8,8,128]{3,2,1,0:T(8,128)} %vel_in.1, s32[8,8]{1,0:T(8,128)} %vmap_in.1, f32[32,8192]{1,0:T(8,128)} %scal_in.1, f32[64,128]{1,0:T(8,128)} %bitcast.9, f32[64,128]{1,0:T(8,128)} %bitcast.10, ...), custom_call_target="tpu_custom_call" | custom-call | tf_op jit(solution)/shard_map/step/pallas_call | solution.py:517
  61.0 1.4 %write_out.1 = (f32[64,128]{1,0:T(8,128)}, f32[64,128]{1,0:T(8,128)}, f32[32,16384]{1,0:T(8,128)}, f32[32,4,128]{2,1,0:T(4,128)}) custom-call(f32[64,128]{1,0:T(8,128)S(1)} %get-tuple-element.12.refs_0_, f32[64,128]{1,0:T(8,128)S(1)} %get-tuple-element.13.refs_1_, f32[32,16384]{1,0:T(8,128)S(1)} %get-tuple-element.14.refs_2_, ...), custom_call_target="tpu_custom_call" | custom-call | tf_op jit(solution)/shard_map/write_out/pallas_call | solution.py:595

commit v4 on v3

--- a/solution.py
+++ b/solution.py
@@ -87,7 +87,7 @@
     ce, cd, ms, mm,
     vel, vmap, scal, mass, pw, cell, mig, rmat, enth,
     hx, hy, ysnd, ypad, q2, q2t, wmat, possend, posrecv, fsend, frecv, bsend, brecv,
-    rows, pt, gbuf, slot, srcv, partv, iacc, bacc, mbuf, tab, frac, found, sendbuf,
+    rows, pt, gbuf, slot, srcv, partv, iacc, sel, bacc, mbuf, tab, frac, found, sendbuf,
     idx_s,
     isem, lsem, xsem, hss, hrs, pss, prs, css, crs, mss, mrs, dss, drs, bss, brs,
 ):
@@ -210,12 +210,31 @@
         axis=1,
     )
 
+    sel[...] = jnp.where(
+        jnp.logical_and(
+            jnp.right_shift(jnp.bitwise_and(iota((256, 512), 0), 127), 5)
+            == jnp.right_shift(iota((256, 512), 1), 7),
+            jnp.bitwise_and(iota((256, 512), 0), 31) == jnp.bitwise_and(iota((256, 512), 1), 31),
+        ),
+        1.0,
+        0.0,
+    ).astype(bf16)
+
+    def spread(b, x):
+        turned = [
+            jnp.concatenate([x[:, 512 * h + 128 * q : 512 * h + 128 * q + 128] for q in range(4)], 0).T
+            for h in range(2)
+        ]
+        out = dot(jnp.concatenate(split2(jnp.concatenate(turned, axis=0)), axis=1), sel[...])
+        for h in range(2):
+            for q in range(4):
+                at = pl.ds(pl.multiple_of(b * 1024 + 512 * h + 128 * q, 128), 128)
+                rows[at, :] = out[128 * h : 128 * h + 128, 128 * q : 128 * q + 128]
+
     def ranks(b, carry):
+        spread(b, scal[:, pl.ds(pl.multiple_of(b * 1024, 1024), 1024)])
         hots = []
         for j in range(8):
-            col = pl.ds(pl.multiple_of((b * 8 + j) * 128, 128), 128)
-            x = scal[:, col]
-            rows[col, :] = jnp.concatenate([x, x, x, x], axis=0).T
             p = mig[pl.ds(b * 8 + j, 1), :]
             hots.append(jnp.where(iota((32, 128), 0) == p, 1.0, 0.0))
         hot = jnp.concatenate(hots, axis=0)
@@ -231,7 +250,7 @@
         slot[r8, :] = mig[r8, :] * CAP + jnp.concatenate(out, axis=0)
         return carry
 
-    lax.fori_loop(0, 8, ranks, jnp.zeros((32, 128), f32))
+    lax.fori_loop(0, 8, ranks, jnp.zeros((32, 128), f32), unroll=2)
 
     for copy in halo:
         copy.wait()
@@ -327,13 +346,12 @@
         for k in range(2):
             b = 2 * i + k
             fetch(partv.at[b], k).wait()
-            before = gbuf[1 - k].T
             gather(k)
-            put_partners(jnp.maximum(b - 1, 0), before)
+            fetch(partv.at[jnp.minimum(b + 2, 14 + k)], k).start()
+            put_partners(b, gbuf[k].T)
             inverse(b)
             if with_lookup:
                 lookup(8 * (b - 8))
-            fetch(partv.at[jnp.minimum(b + 2, 14 + k)], k).start()
         return 0
 
     lax.fori_loop(0, 4, lambda i, _: partners(i, False), 0)
@@ -349,7 +367,6 @@
     lax.fori_loop(4, 8, lambda i, _: partners(i, True), 0)
     for k in range(2):
         fetch(partv.at[14 + k], k).wait()
-    put_partners(15, gbuf[1].T)
 
     inv = iacc[...]
     source = jnp.clip((PD - (inv[:, 0:128] * 128.0 + inv[:, 128:256])).astype(i32), 0, PD)
@@ -381,22 +398,19 @@
 
     def react(b, _):
         mixed = []
-        for j in range(4):
-            c = b * 4 + j
+        for j in range(8):
+            c = b * 8 + j
             col = pl.ds(pl.multiple_of(c * 128, 128), 128)
             s = scal[:, col]
             mixed.append(s + frac[pl.ds(c, 1), :] * (pt[:, col] - s))
         mixed = jnp.concatenate(mixed, axis=1)
         hi, lo = split2(mixed)
         out = mixed + react_step * jnp.tanh(dot(rates, jnp.concatenate([hi, lo, hi], axis=0)))
-        pt[:, pl.ds(pl.multiple_of(b * 512, 512), 512)] = out
-        for j in range(4):
-            x = out[:, 128 * j : 128 * j + 128]
-            col = pl.ds(pl.multiple_of(b * 512 + j * 128, 128), 128)
-            rows[col, :] = jnp.concatenate([x, x, x, x], axis=0).T
+        pt[:, pl.ds(pl.multiple_of(b * 1024, 1024), 1024)] = out
+        spread(b, out)
         return 0
 
-    lax.fori_loop(0, 16, react, 0, unroll=2)
+    lax.fori_loop(0, 8, react, 0, unroll=2)
     rows[PD : PD + 8, :] = jnp.zeros((8, 128), f32)
 
     def slots(d):
@@ -554,6 +568,7 @@
             V((N, 4, 128), i32),
             V((16, 4, 128), i32),
             V((128, 512), f32),
+            V((256, 512), bf16),
             V((64, 512), f32),
             V((N, 4, 128), f32),
             V((128, 128), f32),

time: 62.5 us -> 61.5 us (0.984)
  Pallas kernels: 61.7 us -> 60.7 us
    pallas_call x1, Pallas kernels: 60.3 us -> 59.4 us  [per_device(): pl.pallas_call(kernel, out_shape=(jax.ShapeDtypeStruct((64, 128), f32), j...]
where the time goes in v4:
time: 61.5 us; the launch traced here: 61.4 us
  Pallas kernels  60.7 us (99%)
  between operations  0.64 us (1%)
    pallas_call x1, Pallas kernels, per_device(): pl.pallas_call(kernel, out_shape=(jax.ShapeDtypeStruct((64, 128), f32), j...  59.4 us
    pallas_call x1, Pallas kernels, per_device(): pl.pallas_call(write_out, out_shape=(jax.ShapeDtypeStruct((64, 128), f32)...  1.37 us

profile of v4, /device:TPU:1, one launch (start us, length us, event | category | flops | bytes accessed | tf_op | source)
XLA Modules:
  0.0 61.4 jit_solution(474437880005250280)
XLA Ops:
  0.6 59.4 %step.1 = (f32[64,128]{1,0:T(8,128)S(1)}, f32[64,128]{1,0:T(8,128)S(1)}, f32[32,16384]{1,0:T(8,128)S(1)}, f32[32,4,128]{2,1,0:T(4,128)S(1)}) custom-call(f32[3,8,8,128]{3,2,1,0:T(8,128)} %vel_in.1, s32[8,8]{1,0:T(8,128)} %vmap_in.1, f32[32,8192]{1,0:T(8,128)} %scal_in.1, f32[64,128]{1,0:T(8,128)} %bitcast.9, f32[64,128]{1,0:T(8,128)} %bitcast.10, ...), custom_call_target="tpu_custom_call" | custom-call | tf_op jit(solution)/shard_map/step/pallas_call | solution.py:531
  60.0 1.4 %write_out.1 = (f32[64,128]{1,0:T(8,128)}, f32[64,128]{1,0:T(8,128)}, f32[32,16384]{1,0:T(8,128)}, f32[32,4,128]{2,1,0:T(4,128)}) custom-call(f32[64,128]{1,0:T(8,128)S(1)} %get-tuple-element.12.refs_0_, f32[64,128]{1,0:T(8,128)S(1)} %get-tuple-element.13.refs_1_, f32[32,16384]{1,0:T(8,128)S(1)} %get-tuple-element.14.refs_2_, ...), custom_call_target="tpu_custom_call" | custom-call | tf_op jit(solution)/shard_map/write_out/pallas_call | solution.py:610

commit v5 on v4

--- a/solution.py
+++ b/solution.py
@@ -329,18 +329,22 @@
             pt[:, col] = t[32 * q : 32 * q + 32, :]
 
     def lookup(n0):
-        acc = [found[8 * k : 8 * k + 8, :] for k in range(16)]
+        tables = []
         for j in range(8):
-            om = jnp.broadcast_to(tab[pl.ds(n0 + j, 1), :], (8, 128))
-            ki = jnp.broadcast_to(tab[pl.ds(n0 + j + 64, 1), :], (8, 128))
-            for k in range(8):
-                w = cell[8 * k : 8 * k + 8, :]
-                z = jnp.bitwise_and(w, 127)
-                here = jnp.right_shift(w, 7) == n0 + j
-                acc[k] = jnp.where(here, jnp.take_along_axis(om, z, axis=1), acc[k])
-                acc[8 + k] = jnp.where(here, jnp.take_along_axis(ki, z, axis=1), acc[8 + k])
-        for k in range(16):
-            found[8 * k : 8 * k + 8, :] = acc[k]
+            tables.append(
+                [jnp.broadcast_to(tab[pl.ds(n0 + j + f, 1), :], (8, 128)) for f in (0, 64)]
+            )
+        for k in range(8):
+            w = cell[8 * k : 8 * k + 8, :]
+            z = jnp.bitwise_and(w, 127)
+            n = jnp.right_shift(w, 7) - n0
+            acc = [found[8 * k : 8 * k + 8, :], found[64 + 8 * k : 72 + 8 * k, :]]
+            for j in range(8):
+                here = n == j
+                for f in range(2):
+                    acc[f] = jnp.where(here, jnp.take_along_axis(tables[j][f], z, axis=1), acc[f])
+            found[8 * k : 8 * k + 8, :] = acc[0]
+            found[64 + 8 * k : 72 + 8 * k, :] = acc[1]
 
     def partners(i, with_lookup):
         for k in range(2):
@@ -370,19 +374,8 @@
 
     inv = iacc[...]
     source = jnp.clip((PD - (inv[:, 0:128] * 128.0 + inv[:, 128:256])).astype(i32), 0, PD)
-    moved = inv[:, 256:384] + inv[:, 384:512]
     for p in range(N):
         srcv[p] = source[4 * p : 4 * p + 4, :]
-        mbuf[p] = moved[4 * p : 4 * p + 4, :]
-
-    def send_mass(t, _):
-        p = peer(t)
-        remote(mbuf.at[p], mm.at[me], mss.at[p], mrs.at[me], (p, g)).start()
-        return 0
-
-    lax.fori_loop(1, N, send_mass, 0)
-    own_mass = pltpu.make_async_copy(mbuf.at[me], mm.at[me], lsem.at[4])
-    own_mass.start()
 
     frac[...] = 1.0 - jnp.exp(-mix_step * pw[...] * found[0:64, :])
 
@@ -478,6 +471,19 @@
     )
     bsend[...] = select_dot(wmat[...], table)
     exchange(bsend, brecv, bss, brs, lsem.at[1])
+    moved = iacc[:, 256:384] + iacc[:, 384:512]
+    for p in range(N):
+        mbuf[p] = moved[4 * p : 4 * p + 4, :]
+
+    def send_mass(t, _):
+        p = peer(t)
+        remote(mbuf.at[p], mm.at[me], mss.at[p], mrs.at[me], (p, g)).start()
+        return 0
+
+    lax.fori_loop(1, N, send_mass, 0)
+    own_mass = pltpu.make_async_copy(mbuf.at[me], mm.at[me], lsem.at[4])
+    own_mass.start()
+
     lax.fori_loop(8, 16, lambda i, c: send_pair(i, c, False), peers)
     for k in range(2):
         fetch(srcv.at[me], k).wait()

time: 61.5 us -> 61.1 us (level)
  no operation moved by 1% of the time
where the time goes in v5:
time: 61.1 us; the launch traced here: 61 us
  Pallas kernels  60.4 us (99%)
  between operations  0.64 us (1%)
    pallas_call x1, Pallas kernels, per_device(): pl.pallas_call(kernel, out_shape=(jax.ShapeDtypeStruct((64, 128), f32), j...  59 us
    pallas_call x1, Pallas kernels, per_device(): pl.pallas_call(write_out, out_shape=(jax.ShapeDtypeStruct((64, 128), f32)...  1.37 us

profile of v5, /device:TPU:1, one launch (start us, length us, event | category | flops | bytes accessed | tf_op | source)
XLA Modules:
  0.0 61.0 jit_solution(10268978432218480516)
XLA Ops:
  0.6 59.0 %step.1 = (f32[64,128]{1,0:T(8,128)S(1)}, f32[64,128]{1,0:T(8,128)S(1)}, f32[32,16384]{1,0:T(8,128)S(1)}, f32[32,4,128]{2,1,0:T(4,128)S(1)}) custom-call(f32[3,8,8,128]{3,2,1,0:T(8,128)} %vel_in.1, s32[8,8]{1,0:T(8,128)} %vmap_in.1, f32[32,8192]{1,0:T(8,128)} %scal_in.1, f32[64,128]{1,0:T(8,128)} %bitcast.9, f32[64,128]{1,0:T(8,128)} %bitcast.10, ...), custom_call_target="tpu_custom_call" | custom-call | tf_op jit(solution)/shard_map/step/pallas_call | solution.py:537
  59.6 1.4 %write_out.1 = (f32[64,128]{1,0:T(8,128)}, f32[64,128]{1,0:T(8,128)}, f32[32,16384]{1,0:T(8,128)}, f32[32,4,128]{2,1,0:T(4,128)}) custom-call(f32[64,128]{1,0:T(8,128)S(1)} %get-tuple-element.12.refs_0_, f32[64,128]{1,0:T(8,128)S(1)} %get-tuple-element.13.refs_1_, f32[32,16384]{1,0:T(8,128)S(1)} %get-tuple-element.14.refs_2_, ...), custom_call_target="tpu_custom_call" | custom-call | tf_op jit(solution)/shard_map/write_out/pallas_call | solution.py:616
